TPU v7x, 128 devices: a whole 4x4x4 slice. The times are simulated.
128 devices in a mesh: gx: 8 (over y, core), gy: 4 (over x), gz: 4 (over z).
Axes of the slice: x: 4, y: 4, z: 4, core: 2. Of those that a mesh axis runs over, the one named last changes fastest.
Arguments:
- initial_warmth: float32 [512, 512, 1024], P('gx', 'gy', 'gz'), may hold values from -6 to 6
- heat_supply: float32 [512, 512, 1024], P('gx', 'gy', 'gz'), may hold values from -98304 to 98306
Outputs:
- updated: float32 [512, 512, 1024], P('gx', 'gy', 'gz')
All inputs are finite; a program needn't handle non-finite values.
Results may differ from a plain program's by a relative error of at most 0.0009.
Values sent between devices are 32-bit elements; how exact they have to be, the bound alone decides.
A program may use at most 128 MiB of HBM per device.

v0:
```python
import functools

import jax
import jax.numpy as jnp
import numpy as np
from jax import lax
from jax.experimental import pallas as pl
from jax.experimental.pallas import tpu as pltpu
from jax.sharding import PartitionSpec as P

MESH = pl.DeviceIdType.MESH
HIGH = lax.Precision.HIGHEST
F32 = jnp.float32
BF16 = jnp.bfloat16
LANES = 128
SUB = 8


def generators(whole, factor):
    half = 0.5 * factor
    theta = np.arccosh(1.0 + 0.5 / half)
    scale = np.sqrt(1.0 / (half * np.sinh(theta) * np.sinh((whole + 1) * theta)))
    index = np.arange(whole, dtype=np.float64)
    return np.sinh((index + 1) * theta) * scale, np.sinh((whole - index) * theta) * scale


def diagonal_blocks(u, v, members):
    extent = u.shape[0] // members
    blocks = []
    for member in range(members):
        part = slice(member * extent, (member + 1) * extent)
        own_u, own_v = u[part], v[part]
        lower = np.outer(own_v, own_u)
        blocks.append(np.where(np.tri(extent, dtype=bool), lower, lower.T))
    return np.stack(blocks)


def split_bf16(values):
    high = values.astype(np.float32).astype(BF16)
    low = (values - high.astype(np.float64)).astype(np.float32).astype(BF16)
    return np.asarray(high), np.asarray(low)


def split(values):
    high = values.astype(BF16)
    return high, (values - high.astype(F32)).astype(BF16)


def make_tables(shape, members):
    east, north, upward = shape
    wholes = [extent * count for extent, count in zip(shape, members)]
    factors = [float(whole * whole // 4) for whole in wholes]
    order = np.arange(north)
    order = (north // SUB) * (order % SUB) + order // SUB

    ux, vx = generators(wholes[0], factors[0])
    uy, vy = generators(wholes[1], factors[1])
    uz, vz = generators(wholes[2], factors[2])
    tables = {"factors": factors}
    tables["x"] = np.stack([ux, vx]).astype(np.float32)

    own = [np.stack([w.reshape(members[1], north)[:, order] for w in (uy, vy)], 1)][0]
    tables["y"] = np.repeat(own[..., None], LANES, -1).astype(np.float32)
    by = diagonal_blocks(uy, vy, members[1])[:, order][:, :, order]
    tables["by"] = by.astype(np.float32)
    mom = np.zeros((members[1], 2, 2, north, LANES), np.float32)
    for kind in range(2):
        for m in range(2):
            mom[:, kind, m, :, m] = own[:, kind]
    tables["ymom"] = mom
    wy = np.zeros((members[1], north, LANES), np.float32)
    wy[:, :, 0] = own[:, 1]
    wy[:, :, 1] = own[:, 0]
    tables["wy"] = wy

    bz = diagonal_blocks(uz, vz, members[2])
    tables["bzh"], tables["bzl"] = split_bf16(bz)
    zu, zv = uz.reshape(members[2], upward), vz.reshape(members[2], upward)
    uh, ul = split_bf16(zu)
    vh, vl = split_bf16(zv)
    zero = np.zeros_like(uh)
    tables["zmom"] = np.stack([uh, ul, vh, vl] + [zero] * 12, 1)
    tables["zadd"] = np.stack([vh, vh, vl, uh, uh, ul, zero, zero], 1)
    wz = np.zeros((members[2], LANES, upward), np.float32)
    wz[:, 0] = zv
    wz[:, 1] = zu
    tables["wz"] = wz

    xmom = np.zeros((members[0], 2, 4, SUB, east), np.float32)
    for kind, w in enumerate((ux, vx)):
        for slot in range(4):
            xmom[:, kind, slot, slot] = w.reshape(members[0], east)
    tables["xmom"] = xmom
    return tables


def at(axis, index):
    return {axis: index}


def greet(partners):
    barrier = pltpu.get_barrier_semaphore()
    for partner in partners:
        pl.semaphore_signal(barrier, inc=1, device_id=partner, device_id_type=MESH)
    pl.semaphore_wait(barrier, len(partners))


def remote(src, dst, send, recv, partner):
    return pltpu.make_async_remote_copy(
        src_ref=src, dst_ref=dst, send_sem=send, recv_sem=recv, device_id=partner, device_id_type=MESH
    )


def halo_kernel(sizes, shape, u_ref, hx_ref, hy_ref, send, recv):
    gx, gy = lax.axis_index("gx"), lax.axis_index("gy")
    nx, ny, _ = sizes
    east, north, _ = shape
    xr, xl = lax.rem(gx + 1, nx), lax.rem(gx + nx - 1, nx)
    yr, yl = lax.rem(gy + 1, ny), lax.rem(gy + ny - 1, ny)
    greet([at("gx", xr), at("gx", xl), at("gy", yr), at("gy", yl)])
    copies = [
        remote(u_ref.at[:, north - 1, :], hy_ref.at[0], send.at[2], recv.at[2], at("gy", yr)),
        remote(u_ref.at[:, 0, :], hy_ref.at[1], send.at[3], recv.at[3], at("gy", yl)),
        remote(u_ref.at[east - 1], hx_ref.at[0], send.at[0], recv.at[0], at("gx", xr)),
        remote(u_ref.at[0], hx_ref.at[1], send.at[1], recv.at[1], at("gx", xl)),
    ]
    for copy in copies:
        copy.start()
    for copy in copies:
        copy.wait()


def exchange_halos(u, sizes):
    east, north, upward = u.shape
    vmem = pl.BlockSpec(memory_space=pltpu.VMEM)
    return pl.pallas_call(
        functools.partial(halo_kernel, sizes, u.shape),
        name="halos",
        out_shape=(
            jax.ShapeDtypeStruct((2, north, upward), F32),
            jax.ShapeDtypeStruct((2, east, upward), F32),
        ),
        in_specs=[pl.BlockSpec(memory_space=pl.ANY)],
        out_specs=(vmem, vmem),
        scratch_shapes=[pltpu.SemaphoreType.DMA((4,)), pltpu.SemaphoreType.DMA((4,))],
        compiler_params=pltpu.CompilerParams(collective_id=0, has_side_effects=True),
    )(u)


PLANES = 8
CHUNK = 8


def local_kernel(
    sizes, shape, factors,
    u_ref, s_ref, hx_ref, hy_ref, bzh_ref, bzl_ref, zmom_ref, ytab_ref, xtab_ref,
    g_ref, mx_ref, my_ref, mz_ref,
    u_v, s_v, usem, ssem, gsem,
):
    gx, gy, gz = lax.axis_index("gx"), lax.axis_index("gy"), lax.axis_index("gz")
    nx, ny, _ = sizes
    east, north, upward = shape
    tiles = upward // LANES
    steps = north // SUB
    chunks = east // CHUNK
    rx, ry, _ = factors

    def lanes(l):
        return pl.ds(l * LANES, LANES)

    def loads(c):
        out = []
        rows = pl.ds(c * CHUNK, CHUNK)
        for l in range(tiles):
            out.append(pltpu.make_async_copy(
                u_ref.at[rows, :, lanes(l)], u_v.at[l, pl.ds(1 + c * CHUNK, CHUNK)], usem.at[l, c]))
            out.append(pltpu.make_async_copy(
                s_ref.at[rows, :, lanes(l)], s_v.at[l, rows], ssem.at[l, c]))
        return out

    def stores(c):
        rows = pl.ds(c * CHUNK, CHUNK)
        return [pltpu.make_async_copy(s_v.at[l, rows], g_ref.at[l, rows], gsem.at[l, c]) for l in range(tiles)]

    for c in range(chunks):
        for copy in loads(c):
            copy.start()

    before = jnp.where(gx > 0, 1.0, 0.0).astype(F32)
    after = jnp.where(gx < nx - 1, 1.0, 0.0).astype(F32)
    south = jnp.where(gy > 0, 1.0, 0.0).astype(F32)
    nord = jnp.where(gy < ny - 1, 1.0, 0.0).astype(F32)
    for l in range(tiles):
        u_v[l, 0] = hx_ref[0, :, l * LANES:(l + 1) * LANES] * before
        u_v[l, east + 1] = hx_ref[1, :, l * LANES:(l + 1) * LANES] * after
    mx_ref[...] = jnp.zeros_like(mx_ref)

    bzh, bzl = bzh_ref[gz], bzl_ref[gz]
    zmom = zmom_ref[gz]
    sub = lax.broadcasted_iota(jnp.int32, (SUB, LANES), 0)

    def rows_of(ref, l, i):
        return [ref[l, i, pl.ds(t, SUB, stride=steps), :] for t in range(steps)]

    def stack_rows(rows):
        out = jnp.zeros((SUB, LANES), F32)
        for p, row in enumerate(rows):
            out = jnp.where(sub == p, row, out)
        return out

    def step(b, carry):
        base = pl.multiple_of(b * PLANES, PLANES)
        high, low = [], []
        halo = [
            [hy_ref[side, pl.ds(base, PLANES), l * LANES:(l + 1) * LANES] for l in range(tiles)]
            for side in range(2)
        ]
        for p in range(PLANES):
            i = base + p
            parts = []
            for l in range(tiles):
                col = slice(l * LANES, (l + 1) * LANES)
                u = rows_of(u_v, l, i + 1)
                um = rows_of(u_v, l, i)
                up = rows_of(u_v, l, i + 2)
                s = rows_of(s_v, l, i)
                first = halo[0][l][p:p + 1] * south
                last = halo[1][l][p:p + 1] * nord
                below = jnp.where(sub == 0, first, pltpu.roll(u[-1], 1, 0))
                above = jnp.where(sub == SUB - 1, last, pltpu.roll(u[0], SUB - 1, 0))
                ext = [below] + u + [above]
                f = [
                    s[t] + (2.0 - 2.0 * rx - 2.0 * ry) * u[t]
                    + rx * (um[t] + up[t]) + ry * (ext[t] + ext[t + 2])
                    for t in range(steps)
                ]
                parts.append(jnp.concatenate(f, 0))
            plane = jnp.concatenate(parts, 1)
            h, w = split(plane)
            high.append(h)
            low.append(w)
        high = jnp.concatenate(high, 0)
        low = jnp.concatenate(low, 0)
        y = (
            jnp.dot(high, bzl, preferred_element_type=F32)
            + jnp.dot(low, bzh, preferred_element_type=F32)
            + jnp.dot(high, bzh, preferred_element_type=F32)
        )
        nt = (((1,), (1,)), ((), ()))
        mom = (
            lax.dot_general(zmom, high, nt, preferred_element_type=F32)
            + lax.dot_general(zmom, low, nt, preferred_element_type=F32)
        )
        mu = mom[0:1] + mom[1:2]
        mv = mom[2:3] + mom[3:4]
        for kind, m in enumerate((mu, mv)):
            mz_ref[kind, pl.ds(base, PLANES), :] = stack_rows(
                [m[:, p * north:(p + 1) * north] for p in range(PLANES)])
        for l in range(tiles):
            col = slice(l * LANES, (l + 1) * LANES)
            sums = [[jnp.zeros((SUB, LANES), F32) for _ in range(PLANES)] for _ in range(2)]
            for t in range(steps):
                row = slice(t * SUB, (t + 1) * SUB)
                wu, wv = ytab_ref[gy, 0, row], ytab_ref[gy, 1, row]
                acc_u, acc_v = mx_ref[0, row, col], mx_ref[1, row, col]
                for p in range(PLANES):
                    i = base + p
                    own = u_v[l, i + 1, pl.ds(t, SUB, stride=steps), :]
                    g = y[p * north + t * SUB:p * north + (t + 1) * SUB, col] - 2.0 * own
                    s_v[l, i, row] = g
                    sums[0][p] = sums[0][p] + wu * g
                    sums[1][p] = sums[1][p] + wv * g
                    acc_u = acc_u + xtab_ref[0, gx * east + i] * g
                    acc_v = acc_v + xtab_ref[1, gx * east + i] * g
                mx_ref[0, row, col] = acc_u
                mx_ref[1, row, col] = acc_v
            for kind in range(2):
                my_ref[kind, pl.ds(base, PLANES), col] = stack_rows(
                    [jnp.sum(sums[kind][p], 0, keepdims=True) for p in range(PLANES)])
        return carry

    def chunk(c, carry):
        @pl.when(c < chunks - 1)
        def _():
            for copy in loads(c + 1):
                copy.wait()

        lax.fori_loop(c * (CHUNK // PLANES), (c + 1) * (CHUNK // PLANES), step, 0)
        for copy in stores(c):
            copy.start()
        return carry

    for copy in loads(0):
        copy.wait()
    lax.fori_loop(0, chunks, chunk, 0)
    for c in range(chunks):
        for copy in stores(c):
            copy.wait()


def local_pass(u, s, hx, hy, tables, sizes):
    east, north, upward = u.shape
    tiles = upward // LANES
    chunks = east // CHUNK
    vmem = pl.BlockSpec(memory_space=pltpu.VMEM)
    smem = pl.BlockSpec(memory_space=pltpu.SMEM)
    hbm = pl.BlockSpec(memory_space=pl.ANY)
    return pl.pallas_call(
        functools.partial(local_kernel, sizes, u.shape, tables["factors"]),
        name="local",
        out_shape=(
            jax.ShapeDtypeStruct((tiles, east, north, LANES), F32),
            jax.ShapeDtypeStruct((2, north, upward), F32),
            jax.ShapeDtypeStruct((2, east, upward), F32),
            jax.ShapeDtypeStruct((2, east, north), F32),
        ),
        in_specs=[hbm, hbm, vmem, vmem, vmem, vmem, vmem, vmem, smem],
        out_specs=(hbm, vmem, vmem, vmem),
        scratch_shapes=[
            pltpu.VMEM((tiles, east + 2, north, LANES), F32),
            pltpu.VMEM((tiles, east, north, LANES), F32),
            pltpu.SemaphoreType.DMA((tiles, chunks)),
            pltpu.SemaphoreType.DMA((tiles, chunks)),
            pltpu.SemaphoreType.DMA((tiles, chunks)),
        ],
    )(u, s, hx, hy, tables["bzh"], tables["bzl"], tables["zmom"], tables["y"], tables["x"])


def couple_kernel(
    sizes, shape,
    mx_ref, my_ref, mz_ref, ymom_ref, wy_ref, wz_ref, by_ref, xmom_ref,
    cz_ref, cy_ref, cx_ref,
    zbuf, ybuf, xpair, xtot, xbuf, xback, eown, ebuf, town, tbuf,
    zs, zr, ys, yr, ps, pr, xs, xr, bs, br, es, er, ts, tr,
):
    gx, gy, gz = lax.axis_index("gx"), lax.axis_index("gy"), lax.axis_index("gz")
    nx, ny, nz = sizes
    east, north, upward = shape
    chips = nx // 2
    half = north // 2
    chip, core = gx // 2, lax.rem(gx, 2)
    mine = pl.ds(pl.multiple_of(core * half, half), half)
    theirs = pl.ds(pl.multiple_of((1 - core) * half, half), half)
    partner = at("gx", chip * 2 + 1 - core)

    def ring(axis, me, count):
        return [at(axis, lax.rem(me + o, count)) for o in range(1, count)]

    greet(ring("gx", gx, nx) + ring("gy", gy, ny) + ring("gz", gz, nz))

    def kind_to(me, count, o):
        return jnp.where(lax.rem(me + o, count) > me, 0, 1)

    def from_below(me, count, o):
        return jnp.where(lax.rem(me + count - o, count) < me, 1.0, 0.0).astype(F32)

    def gather(me, count, buf):
        left = right = None
        for o in range(1, count):
            low = from_below(me, count, o)
            piece = buf[o - 1]
            left = piece * low if left is None else left + piece * low
            right = piece * (1.0 - low) if right is None else right + piece * (1.0 - low)
        return left, right

    pair = remote(mx_ref.at[:, theirs, :], xpair, ps, pr, partner)
    pair.start()
    zcopies = [
        remote(mz_ref.at[kind_to(gz, nz, o)], zbuf.at[o - 1], zs.at[o - 1], zr.at[o - 1],
               at("gz", lax.rem(gz + o, nz)))
        for o in range(1, nz)
    ]
    for copy in zcopies:
        copy.start()
    ycopies = [
        remote(my_ref.at[kind_to(gy, ny, o)], ybuf.at[o - 1], ys.at[o - 1], yr.at[o - 1],
               at("gy", lax.rem(gy + o, ny)))
        for o in range(1, ny)
    ]
    for copy in ycopies:
        copy.start()
    pair.wait()
    xtot[0] = mx_ref[0, mine, :] + xpair[0]
    xtot[1] = mx_ref[1, mine, :] + xpair[1]
    xcopies = [
        remote(xtot.at[kind_to(chip, chips, o)], xbuf.at[o - 1], xs.at[o - 1], xr.at[o - 1],
               at("gx", lax.rem(chip + o, chips) * 2 + core))
        for o in range(1, chips)
    ]
    for copy in xcopies:
        copy.start()

    for copy in zcopies:
        copy.wait()
    pz, sz = gather(gz, nz, zbuf)

    def pack(value, base):
        high = value.astype(BF16).astype(F32)
        low = (value - high).astype(BF16).astype(F32)
        cz_ref[:, base, :] = high
        cz_ref[:, base + 1, :] = low
        cz_ref[:, base + 2, :] = high

    pack(pz, 0)
    pack(sz, 3)
    cz_ref[:, 6, :] = jnp.zeros_like(pz)
    cz_ref[:, 7, :] = jnp.zeros_like(pz)

    def dot(a, b, dims=(((1,), (0,)), ((), ()))):
        return lax.dot_general(a, b, dims, precision=HIGH, preferred_element_type=F32)

    for kind in range(2):
        eown[kind] = dot(pz, ymom_ref[gy, kind, 0]) + dot(sz, ymom_ref[gy, kind, 1])
    ecopies = [
        remote(eown.at[kind_to(gy, ny, o)], ebuf.at[o - 1], es.at[o - 1], er.at[o - 1],
               at("gy", lax.rem(gy + o, ny)))
        for o in range(1, ny)
    ]
    for copy in ecopies:
        copy.start()

    for copy in ycopies:
        copy.wait()
    left, right = gather(gy, ny, ybuf)
    for copy in ecopies:
        copy.wait()
    eleft, eright = gather(gy, ny, ebuf)
    wz = wz_ref[gz]
    py = left + dot(eleft, wz)
    sy = right + dot(eright, wz)
    cy_ref[0] = py
    cy_ref[1] = sy

    for kind in range(2):
        town[kind, :, 0:upward] = (
            dot(xmom_ref[gx, kind, 0], py) + dot(xmom_ref[gx, kind, 1], sy))
        town[kind, :, upward:] = (
            dot(xmom_ref[gx, kind, 0], pz) + dot(xmom_ref[gx, kind, 1], sz))
    tcopies = [
        remote(town.at[kind_to(gx, nx, o)], tbuf.at[o - 1], ts.at[o - 1], tr.at[o - 1],
               at("gx", lax.rem(gx + o, nx)))
        for o in range(1, nx)
    ]
    for copy in tcopies:
        copy.start()

    for copy in xcopies:
        copy.wait()
    px, sx = gather(chip, chips, xbuf)
    first = jnp.where(core == 0, 1.0, 0.0).astype(F32)
    second = 1.0 - first
    xback[0] = px + first * mx_ref[0, mine, :]
    xback[1] = sx + second * mx_ref[1, mine, :]
    back = remote(xback, cx_ref.at[:, mine, :], bs, br, partner)
    back.start()
    cx_ref[0, mine, :] = px + second * xpair[0]
    cx_ref[1, mine, :] = sx + first * xpair[1]

    for copy in tcopies:
        copy.wait()
    tleft, tright = gather(gx, nx, tbuf)
    tright = tright + town[1]
    by = by_ref[gy]
    wy = wy_ref[gy][:, 0:SUB]
    back.wait()
    for kind, edge in ((0, tleft), (1, tright)):
        face = cx_ref[kind]
        if kind == 1:
            face = face + mx_ref[1]
        folded = dot(edge[:, upward:], by)
        cx_ref[kind] = (
            dot(by, face)
            + dot(wy, edge[:, 0:upward])
            + dot(folded, wz[0:SUB], (((0,), (0,)), ((), ())))
        )


def couple(mx, my, mz, tables, shape, sizes):
    east, north, upward = shape
    nx, ny, nz = sizes
    chips = nx // 2
    vmem = pl.BlockSpec(memory_space=pltpu.VMEM)
    dma = pltpu.SemaphoreType.DMA
    half = north // 2
    return pl.pallas_call(
        functools.partial(couple_kernel, sizes, shape),
        name="couple",
        out_shape=(
            jax.ShapeDtypeStruct((east, SUB, north), F32),
            jax.ShapeDtypeStruct((2, east, upward), F32),
            jax.ShapeDtypeStruct((2, north, upward), F32),
        ),
        in_specs=[vmem] * 8,
        out_specs=(vmem, vmem, vmem),
        scratch_shapes=[
            pltpu.VMEM((nz - 1, east, north), F32),
            pltpu.VMEM((ny - 1, east, upward), F32),
            pltpu.VMEM((2, half, upward), F32),
            pltpu.VMEM((2, half, upward), F32),
            pltpu.VMEM((chips - 1, half, upward), F32),
            pltpu.VMEM((2, half, upward), F32),
            pltpu.VMEM((2, east, LANES), F32),
            pltpu.VMEM((ny - 1, east, LANES), F32),
            pltpu.VMEM((2, SUB, upward + north), F32),
            pltpu.VMEM((nx - 1, SUB, upward + north), F32),
            dma((nz - 1,)), dma((nz - 1,)),
            dma((ny - 1,)), dma((ny - 1,)),
            dma, dma,
            dma((chips - 1,)), dma((chips - 1,)),
            dma, dma,
            dma((ny - 1,)), dma((ny - 1,)),
            dma((nx - 1,)), dma((nx - 1,)),
        ],
        compiler_params=pltpu.CompilerParams(collective_id=1, has_side_effects=True),
    )(mx, my, mz, tables["ymom"], tables["wy"], tables["wz"], tables["by"], tables["xmom"])


def final_kernel(
    shape,
    g_ref, u_ref, cz_ref, cy_ref, cx_ref, zadd_ref, ytab_ref, xtab_ref,
    o_ref,
    g_v, u_v, o_v, gsem, usem, osem,
):
    gx, gy, gz = lax.axis_index("gx"), lax.axis_index("gy"), lax.axis_index("gz")
    east, north, upward = shape
    tiles = upward // LANES
    steps = north // SUB
    chunks = east // CHUNK

    def lanes(l):
        return pl.ds(l * LANES, LANES)

    def loads(c):
        out = []
        rows = pl.ds(c * CHUNK, CHUNK)
        for l in range(tiles):
            out.append(pltpu.make_async_copy(g_ref.at[l, rows], g_v.at[l, rows], gsem.at[l, c]))
            out.append(pltpu.make_async_copy(
                u_ref.at[rows, :, lanes(l)], u_v.at[l, rows], usem.at[l, c]))
        return out

    def stores(c):
        rows = pl.ds(c * CHUNK, CHUNK)
        return [
            pltpu.make_async_copy(o_v.at[l, rows], o_ref.at[rows, :, lanes(l)], osem.at[l, c])
            for l in range(tiles)
        ]

    for c in range(chunks):
        for copy in loads(c):
            copy.start()

    zadd = zadd_ref[gz]
    sub = lax.broadcasted_iota(jnp.int32, (SUB, LANES), 0)

    def scan(value, backward):
        def shifted(x, d):
            if backward:
                return jnp.where(sub < SUB - d, pltpu.roll(x, SUB - d, 0), 0.0)
            return jnp.where(sub >= d, pltpu.roll(x, d, 0), 0.0)

        for d in (1, 2, 4):
            value = value + shifted(value, d)
        return shifted(value, 1)

    def step(b, carry):
        base = pl.multiple_of(b * PLANES, PLANES)
        add = []
        for p in range(PLANES):
            cz = cz_ref[base + p].T.astype(BF16)
            add.append(jnp.dot(cz, zadd, preferred_element_type=F32))
        for l in range(tiles):
            col = slice(l * LANES, (l + 1) * LANES)
            edge = [cy_ref[kind, pl.ds(base, PLANES), col] for kind in range(2)]
            for p in range(PLANES):
                i = base + p
                g = []
                for t in range(steps):
                    row = slice(t * SUB, (t + 1) * SUB)
                    g.append(g_v[l, i, row] + add[p][row, col])
                su = sv = None
                for t in range(steps):
                    row = slice(t * SUB, (t + 1) * SUB)
                    pu = ytab_ref[gy, 0, row] * g[t]
                    pv = ytab_ref[gy, 1, row] * g[t]
                    su = pu if su is None else su + pu
                    sv = pv if sv is None else sv + pv
                below = scan(su, False) + edge[0][p:p + 1]
                above = scan(sv, True) + edge[1][p:p + 1] + sv
                for t in range(steps):
                    row = slice(t * SUB, (t + 1) * SUB)
                    wu, wv = ytab_ref[gy, 0, row], ytab_ref[gy, 1, row]
                    below = below + wu * g[t]
                    above = above - wv * g[t]
                    g_v[l, i, row] = wv * below + wu * above
            for t in range(steps):
                row = slice(t * SUB, (t + 1) * SUB)
                below, above = cx_ref[0, row, col], cx_ref[1, row, col]
                for p in range(PLANES):
                    i = base + p
                    wu, wv = xtab_ref[0, gx * east + i], xtab_ref[1, gx * east + i]
                    h = g_v[l, i, row]
                    below = below + wu * h
                    above = above - wv * h
                    own = u_v[l, i, pl.ds(t, SUB, stride=steps), :]
                    o_v[l, i, pl.ds(t, SUB, stride=steps), :] = own + (wv * below + wu * above)
                cx_ref[0, row, col] = below
                cx_ref[1, row, col] = above
        return carry

    def chunk(c, carry):
        for copy in loads(c):
            copy.wait()
        lax.fori_loop(c * (CHUNK // PLANES), (c + 1) * (CHUNK // PLANES), step, 0)
        for copy in stores(c):
            copy.start()
        return carry

    lax.fori_loop(0, chunks, chunk, 0)
    for c in range(chunks):
        for copy in stores(c):
            copy.wait()


def final_outer(shape, g_ref, u_ref, cz_ref, cy_ref, cxin_ref, zadd_ref, ytab_ref, xtab_ref, o_ref, cx_v, *rest):
    cx_v[...] = cxin_ref[...]
    final_kernel(shape, g_ref, u_ref, cz_ref, cy_ref, cx_v, zadd_ref, ytab_ref, xtab_ref, o_ref, *rest)


def final_pass(g, u, cz, cy, cx, tables):
    east, north, upward = u.shape
    tiles = upward // LANES
    chunks = east // CHUNK
    vmem = pl.BlockSpec(memory_space=pltpu.VMEM)
    smem = pl.BlockSpec(memory_space=pltpu.SMEM)
    hbm = pl.BlockSpec(memory_space=pl.ANY)
    block = pltpu.VMEM((tiles, east, north, LANES), F32)
    return pl.pallas_call(
        functools.partial(final_outer, u.shape),
        name="final",
        out_shape=jax.ShapeDtypeStruct(u.shape, F32),
        in_specs=[hbm, hbm, vmem, vmem, vmem, vmem, vmem, smem],
        out_specs=hbm,
        scratch_shapes=[
            pltpu.VMEM((2, north, upward), F32),
            block, block, block,
            pltpu.SemaphoreType.DMA((tiles, chunks)),
            pltpu.SemaphoreType.DMA((tiles, chunks)),
            pltpu.SemaphoreType.DMA((tiles, chunks)),
        ],
    )(g, u, cz, cy, cx, tables["zadd"], tables["y"], tables["x"])


def local(sizes, u, s):
    tables = make_tables(u.shape, sizes)
    hx, hy = exchange_halos(u, sizes)
    g, mx, my, mz = local_pass(u, s, hx, hy, tables, sizes)
    cz, cy, cx = couple(mx, my, mz, tables, u.shape, sizes)
    return final_pass(g, u, cz, cy, cx, tables)


def solution(mesh):
    sizes = tuple(mesh.shape[name] for name in ("gx", "gy", "gz"))
    spec = P("gx", "gy", "gz")
    return jax.shard_map(
        functools.partial(local, sizes), mesh=mesh, in_specs=(spec, spec), out_specs=spec, check_vma=False
    )
```

profile of v0, /device:TPU:1, one launch (start us, length us, event | category | flops | bytes accessed | tf_op | source)
XLA Modules:
  0.0 66.5 jit_solution(12598327928299075674)
XLA Ops:
  0.0 9.5 %halos.1 = (f32[2,128,256]{2,1,0:T(8,128)}, f32[2,64,256]{2,1,0:T(8,128)}) custom-call(f32[64,128,256]{2,1,0:T(8,128)} %u_ref.5), custom_call_target="tpu_custom_call" | custom-call | tf_op jit(solution)/shard_map/halos/pallas_call | solution.py:136
  9.5 20.2 %local.1 = (f32[2,64,128,128]{3,2,1,0:T(8,128)}, f32[2,128,256]{2,1,0:T(8,128)}, f32[2,64,256]{2,1,0:T(8,128)}, f32[2,64,128]{2,1,0:T(8,128)}) custom-call(f32[64,128,256]{2,1,0:T(8,128)} %u_ref.5, f32[64,128,256]{2,1,0:T(8,128)} %s_ref.1, f32[2,128,256]{2,1,0:T(8,128)} %get-tuple-element.14.hx_ref, f32[2,64,256]{2,1,0:T(8,128)} %get-tuple-element.15.hy_ref, ...), custom_call_target="tpu_custom_call" | custom-call | tf_op jit(solution)/shard_map/local/pallas_call | solution.py:308
  29.8 21.3 %couple.1 = (f32[64,8,128]{2,1,0:T(8,128)}, f32[2,64,256]{2,1,0:T(8,128)}, f32[2,128,256]{2,1,0:T(8,128)}) custom-call(f32[2,128,256]{2,1,0:T(8,128)} %get-tuple-element.17.mx_ref, f32[2,64,256]{2,1,0:T(8,128)} %get-tuple-element.18.my_ref, f32[2,64,128]{2,1,0:T(8,128)} %get-tuple-element.19.mz_ref, f32[4,2,2,128,128]{4,3,2,1,0:T(8,128)} %constant.27.clone.ymom_ref, ...), custom_call_target="tpu_custom_call" | custom-call | tf_op jit(solution)/shard_map/couple/pallas_call | solution.py:485
  51.0 15.5 %final.1 = f32[64,128,256]{2,1,0:T(8,128)} custom-call(f32[2,64,128,128]{3,2,1,0:T(8,128)} %get-tuple-element.16.g_ref, f32[64,128,256]{2,1,0:T(8,128)} %u_ref.5, f32[64,8,128]{2,1,0:T(8,128)} %get-tuple-element.20.cz_ref, f32[2,64,256]{2,1,0:T(8,128)} %get-tuple-element.21.cy_ref, f32[2,128,256]{2,1,0:T(8,128)} %get-tuple-element.22.cxin_ref, ...), custom_call_target="tpu_custom_call" | custom-call | tf_op jit(solution)/shard_map/final/pallas_call | solution.py:638
where the time goes:
time: 66.7 us; the launch traced here: 66.5 us
  Pallas kernels  66.5 us (100%)
    pallas_call x1, Pallas kernels, couple(): pl.pallas_call(functools.partial(couple_kernel, sizes, shape), name='coup...  21.3 us
    pallas_call x1, Pallas kernels, local_pass(): pl.pallas_call(functools.partial(local_kernel, sizes, u.shape, tables['fa...  20.2 us
    pallas_call x1, Pallas kernels, final_pass(): pl.pallas_call(functools.partial(final_outer, u.shape), name='final', out...  15.5 us
    pallas_call x1, Pallas kernels, exchange_halos(): pl.pallas_call(functools.partial(halo_kernel, sizes, u.shape), name='halo...  9.5 us

commit v1 on v0

v1 whole, which is shorter than its diff:
```python
import functools

import jax
import jax.numpy as jnp
import numpy as np
from jax import lax
from jax.experimental import pallas as pl
from jax.experimental.pallas import tpu as pltpu
from jax.sharding import PartitionSpec as P

MESH = pl.DeviceIdType.MESH
HIGH = lax.Precision.HIGHEST
F32 = jnp.float32
BF16 = jnp.bfloat16
LANES = 128
SUB = 8


def generators(whole, factor):
    half = 0.5 * factor
    theta = np.arccosh(1.0 + 0.5 / half)
    scale = np.sqrt(1.0 / (half * np.sinh(theta) * np.sinh((whole + 1) * theta)))
    index = np.arange(whole, dtype=np.float64)
    return np.sinh((index + 1) * theta) * scale, np.sinh((whole - index) * theta) * scale


def diagonal_blocks(u, v, members):
    extent = u.shape[0] // members
    blocks = []
    for member in range(members):
        part = slice(member * extent, (member + 1) * extent)
        own_u, own_v = u[part], v[part]
        lower = np.outer(own_v, own_u)
        blocks.append(np.where(np.tri(extent, dtype=bool), lower, lower.T))
    return np.stack(blocks)


def split_bf16(values):
    high = values.astype(np.float32).astype(BF16)
    low = (values - high.astype(np.float64)).astype(np.float32).astype(BF16)
    return np.asarray(high), np.asarray(low)


def split(values):
    high = values.astype(BF16)
    return high, (values - high.astype(F32)).astype(BF16)


def make_tables(shape, members):
    east, north, upward = shape
    wholes = [extent * count for extent, count in zip(shape, members)]
    factors = [float(whole * whole // 4) for whole in wholes]
    order = np.arange(north)
    order = (north // SUB) * (order % SUB) + order // SUB

    ux, vx = generators(wholes[0], factors[0])
    uy, vy = generators(wholes[1], factors[1])
    uz, vz = generators(wholes[2], factors[2])
    tables = {"factors": factors}
    tables["x"] = np.stack([ux, vx]).astype(np.float32)

    own = np.stack([w.reshape(members[1], north)[:, order] for w in (uy, vy)], 1)
    tables["y"] = np.repeat(own[..., None], LANES, -1).astype(np.float32)
    by = diagonal_blocks(uy, vy, members[1])[:, order][:, :, order]
    tables["by"] = by.astype(np.float32)
    tables["bx"] = diagonal_blocks(ux, vx, members[0]).astype(np.float32)
    yw = np.zeros((members[1], 2, 2, SUB, north), np.float32)
    xw = np.zeros((members[0], 2, 2, SUB, east), np.float32)
    for slot in range(2):
        yw[:, :, slot, slot] = own
        for kind, w in enumerate((ux, vx)):
            xw[:, kind, slot, slot] = w.reshape(members[0], east)
    tables["yw"], tables["xw"] = yw, xw
    wy = np.zeros((members[1], SUB, north), np.float32)
    wy[:, 0] = own[:, 1]
    wy[:, 1] = own[:, 0]
    tables["wy"] = wy

    bzh, bzl = split_bf16(diagonal_blocks(uz, vz, members[2]))
    tables["bz"] = np.stack([bzh, bzl], 1)
    zu, zv = uz.reshape(members[2], upward), vz.reshape(members[2], upward)
    uh, ul = split_bf16(zu)
    vh, vl = split_bf16(zv)
    zero = np.zeros_like(uh)
    tables["zmom"] = np.stack([uh, ul, vh, vl] + [zero] * 12, 1)
    tables["zadd"] = np.stack([vh, vh, vl, uh, uh, ul, zero, zero], 1)
    return tables


def at(axis, index):
    return {axis: index}


def greet(partners):
    barrier = pltpu.get_barrier_semaphore()
    for partner in partners:
        pl.semaphore_signal(barrier, inc=1, device_id=partner, device_id_type=MESH)
    pl.semaphore_wait(barrier, len(partners))


def remote(src, dst, send, recv, partner):
    return pltpu.make_async_remote_copy(
        src_ref=src, dst_ref=dst, send_sem=send, recv_sem=recv, device_id=partner, device_id_type=MESH
    )


def kind_to(me, count, o):
    return jnp.where(lax.rem(me + o, count) > me, 0, 1)


def gather(me, count, buf):
    left = right = None
    for o in range(1, count):
        low = jnp.where(lax.rem(me + count - o, count) < me, 1.0, 0.0).astype(F32)
        piece = buf[o - 1]
        left = piece * low if left is None else left + piece * low
        right = piece * (1.0 - low) if right is None else right + piece * (1.0 - low)
    return left, right


NN = (((1,), (0,)), ((), ()))
NT = (((1,), (1,)), ((), ()))
TN = (((0,), (0,)), ((), ()))


def dot(a, b, dims=NN):
    return lax.dot_general(a, b, dims, precision=HIGH, preferred_element_type=F32)


PLANES = 8


def stack_rows(rows, width=LANES):
    sub = lax.broadcasted_iota(jnp.int32, (SUB, width), 0)
    out = jnp.zeros((SUB, width), F32)
    for p, row in enumerate(rows):
        out = jnp.where(sub == p, row, out)
    return out


def local_kernel(
    sizes, shape, factors,
    u_ref, s_ref, bz_ref, zmom_ref, ytab_ref, yw_ref, xw_ref, wy_ref, by_ref, bx_ref, xtab_ref,
    g_ref, sg_ref, cz_ref, cy_ref, cx_ref,
    u_v, s_v, fh, fl, hx, hy, mxf, mxu, mx, my, mz,
    zbuf, zpad, ybuf, xpair, xtot, xbuf, xback, eown, ebuf, qown, qbuf, rown, rbuf, town, tbuf,
    usem, ssem, gsem, hs, hr, zs, zr, ys, yr, ps, pr, xs, xr, bs, br, es, er, qs, qr, rs, rr, ts, tr,
):
    gx, gy, gz = lax.axis_index("gx"), lax.axis_index("gy"), lax.axis_index("gz")
    nx, ny, nz = sizes
    east, north, upward = shape
    tiles = upward // LANES
    steps = north // SUB
    chunks = east // PLANES
    rx, ry, _ = factors
    chips = nx // 2
    half = north // 2
    chip, core = gx // 2, lax.rem(gx, 2)
    mine = pl.ds(pl.multiple_of(core * half, half), half)
    theirs = pl.ds(pl.multiple_of((1 - core) * half, half), half)
    partner = at("gx", chip * 2 + 1 - core)

    def lanes(l):
        return pl.ds(l * LANES, LANES)

    def u_loads(c):
        rows = pl.ds(c * PLANES, PLANES)
        return [
            pltpu.make_async_copy(
                u_ref.at[rows, :, lanes(l)], u_v.at[l, pl.ds(1 + c * PLANES, PLANES)], usem.at[l, c])
            for l in range(tiles)
        ]

    def s_loads(c):
        rows = pl.ds(c * PLANES, PLANES)
        return [
            pltpu.make_async_copy(s_ref.at[rows, :, lanes(l)], s_v.at[l, rows], ssem.at[l, c])
            for l in range(tiles)
        ]

    def g_stores(c):
        rows = pl.ds(c * PLANES, PLANES)
        return [pltpu.make_async_copy(s_v.at[l, rows], g_ref.at[l, rows], gsem.at[l, c]) for l in range(tiles)]

    for loads in (u_loads, s_loads):
        for c in range(chunks):
            for copy in loads(c):
                copy.start()

    def ring(axis, me, count):
        return [at(axis, lax.rem(me + o, count)) for o in range(1, count)]

    greet(ring("gx", gx, nx) + ring("gy", gy, ny) + ring("gz", gz, nz))

    xr_, xl_ = lax.rem(gx + 1, nx), lax.rem(gx + nx - 1, nx)
    yr_, yl_ = lax.rem(gy + 1, ny), lax.rem(gy + ny - 1, ny)
    halos = [
        remote(u_ref.at[:, north - 1, :], hy.at[0], hs.at[2], hr.at[2], at("gy", yr_)),
        remote(u_ref.at[:, 0, :], hy.at[1], hs.at[3], hr.at[3], at("gy", yl_)),
        remote(u_ref.at[east - 1], hx.at[0], hs.at[0], hr.at[0], at("gx", xr_)),
        remote(u_ref.at[0], hx.at[1], hs.at[1], hr.at[1], at("gx", xl_)),
    ]
    for copy in halos:
        copy.start()

    sub = lax.broadcasted_iota(jnp.int32, (SUB, LANES), 0)

    def cols(l):
        return slice(l * LANES, (l + 1) * LANES)

    def rows_at(t):
        return slice(t * SUB, (t + 1) * SUB)

    def strided(t):
        return pl.ds(t, SUB, stride=steps)

    mxu[...] = jnp.zeros_like(mxu)
    mxf[...] = jnp.zeros_like(mxf)
    zpad[...] = jnp.zeros_like(zpad)

    def weights(base):
        return [[xtab_ref[kind, gx * east + base + p] for p in range(PLANES)] for kind in range(2)]

    def pre(c, carry):
        for copy in u_loads(c):
            copy.wait()
        base = c * PLANES
        w = weights(base)
        for l in range(tiles):
            for t in range(steps):
                acc = [mxu[kind, rows_at(t), cols(l)] for kind in range(2)]
                for p in range(PLANES):
                    own = u_v[l, base + p + 1, strided(t), :]
                    for kind in range(2):
                        acc[kind] = acc[kind] + w[kind][p] * own
                for kind in range(2):
                    mxu[kind, rows_at(t), cols(l)] = acc[kind]
        return carry

    lax.fori_loop(0, chunks, pre, 0)

    for copy in halos:
        copy.wait()
    before = jnp.where(gx > 0, 1.0, 0.0).astype(F32)
    after = jnp.where(gx < nx - 1, 1.0, 0.0).astype(F32)
    south = jnp.where(gy > 0, 1.0, 0.0).astype(F32)
    nord = jnp.where(gy < ny - 1, 1.0, 0.0).astype(F32)
    for l in range(tiles):
        u_v[l, 0] = hx[0, :, cols(l)] * before
        u_v[l, east + 1] = hx[1, :, cols(l)] * after

    zmom = zmom_ref[gz]

    def z_moments(c):
        base = pl.multiple_of(c * PLANES, PLANES)
        mom = None
        for f in (fh, fl):
            flat = f[pl.ds(base, PLANES)].reshape(PLANES * north, upward)
            part = lax.dot_general(zmom, flat, NT, preferred_element_type=F32)
            mom = part if mom is None else mom + part
        for kind in range(2):
            m = mom[2 * kind:2 * kind + 1] + mom[2 * kind + 1:2 * kind + 2]
            mz[kind, pl.ds(base, PLANES), :] = stack_rows(
                [m[:, p * north:(p + 1) * north] for p in range(PLANES)])

    def rhs(c, carry):
        for copy in s_loads(c):
            copy.wait()
        base = pl.multiple_of(c * PLANES, PLANES)
        w = weights(base)
        for l in range(tiles):
            col = cols(l)
            edge = [hy[0, pl.ds(base, PLANES), col] * south, hy[1, pl.ds(base, PLANES), col] * nord]
            for t2 in range(0, steps, 2):
                acc = [[mxf[kind, rows_at(t2 + k), col] for k in range(2)] for kind in range(2)]
                column = [[u_v[l, base + p, strided(t2 + k), :] for p in range(PLANES + 2)] for k in range(2)]
                for p in range(PLANES):
                    i = base + p
                    if t2 == 0:
                        below = pltpu.roll(u_v[l, i + 1, strided(steps - 1), :], 1, 0)
                        below = jnp.where(sub == 0, edge[0][p:p + 1], below)
                    else:
                        below = u_v[l, i + 1, strided(t2 - 1), :]
                    if t2 == steps - 2:
                        above = pltpu.roll(u_v[l, i + 1, strided(0), :], SUB - 1, 0)
                        above = jnp.where(sub == SUB - 1, edge[1][p:p + 1], above)
                    else:
                        above = u_v[l, i + 1, strided(t2 + 2), :]
                    out = []
                    for k in range(2):
                        own = column[k][p + 1]
                        across = column[k][p] + column[k][p + 2]
                        along = (below + column[1][p + 1]) if k == 0 else (column[0][p + 1] + above)
                        if rx == ry:
                            spread = rx * ((across + along) + (2.0 / rx - 4.0) * own)
                        else:
                            spread = rx * across + ry * along + (2.0 - 2.0 * rx - 2.0 * ry) * own
                        f = s_v[l, i, strided(t2 + k), :] + spread
                        for kind in range(2):
                            acc[kind][k] = acc[kind][k] + w[kind][p] * f
                        out.append(f)
                    pair = jnp.concatenate(out, 0)
                    high = pair.astype(BF16)
                    rows = slice(t2 * SUB, (t2 + 2) * SUB)
                    fh[i, rows, col] = high
                    fl[i, rows, col] = (pair - high.astype(F32)).astype(BF16)
                for kind in range(2):
                    for k in range(2):
                        mxf[kind, rows_at(t2 + k), col] = acc[kind][k]
        z_moments(c)
        return carry

    lax.fori_loop(0, chunks, rhs, 0)

    zcopies = [
        remote(mz.at[kind_to(gz, nz, o)], zbuf.at[o - 1], zs.at[o - 1], zr.at[o - 1],
               at("gz", lax.rem(gz + o, nz)))
        for o in range(1, nz)
    ]
    for copy in zcopies:
        copy.start()

    def solve_up(high, low):
        stack = jnp.concatenate([bz_ref[gz, 1], bz_ref[gz, 0], bz_ref[gz, 0]], 0)
        return jnp.dot(jnp.concatenate([high, low, high], 1), stack, preferred_element_type=F32)

    fold_h, fold_l = split(mxf[...].reshape(2 * north, upward))
    mx[...] = solve_up(fold_h, fold_l).reshape(2, north, upward) - 2.0 * mxu[...]

    pair = remote(mx.at[:, theirs, :], xpair, ps, pr, partner)
    pair.start()
    for kind in range(2):
        qown[kind] = dot(yw_ref[gy, kind, 0], mx[0]) + dot(yw_ref[gy, kind, 1], mx[1])
    qcopies = [
        remote(qown.at[kind_to(gy, ny, o)], qbuf.at[o - 1], qs.at[o - 1], qr.at[o - 1],
               at("gy", lax.rem(gy + o, ny)))
        for o in range(1, ny)
    ]
    for copy in qcopies:
        copy.start()
    xcopies = [
        remote(xtot.at[kind_to(chip, chips, o)], xbuf.at[o - 1], xs.at[o - 1], xr.at[o - 1],
               at("gx", lax.rem(chip + o, chips) * 2 + core))
        for o in range(1, chips)
    ]
    rcopies = [
        remote(rown.at[kind_to(gx, nx, o)], rbuf.at[o - 1], rs.at[o - 1], rr.at[o - 1],
               at("gx", lax.rem(gx + o, nx)))
        for o in range(1, nx)
    ]

    def send_chips():
        pair.wait()
        xtot[0] = mx[0, mine, :] + xpair[0]
        xtot[1] = mx[1, mine, :] + xpair[1]
        for copy in xcopies:
            copy.start()

    def send_edges():
        for copy in qcopies:
            copy.wait()
        qleft, qright = gather(gy, ny, qbuf)
        for kind in range(2):
            rown[kind] = stack_rows([qleft[kind:kind + 1], qright[kind:kind + 1]], upward)
        for copy in rcopies:
            copy.start()

    def solve(c, carry):
        base = pl.multiple_of(c * PLANES, PLANES)

        @pl.when(c == min(2, chunks - 1))
        def _():
            send_chips()

        @pl.when(c == min(5, chunks - 1))
        def _():
            send_edges()

        y = solve_up(
            fh[pl.ds(base, PLANES)].reshape(PLANES * north, upward),
            fl[pl.ds(base, PLANES)].reshape(PLANES * north, upward),
        )
        for l in range(tiles):
            col = cols(l)
            sums = [[None] * PLANES for _ in range(2)]
            for t in range(steps):
                w = [ytab_ref[gy, kind, rows_at(t)] for kind in range(2)]
                for p in range(PLANES):
                    i = base + p
                    own = u_v[l, i + 1, strided(t), :]
                    g = y[p * north + t * SUB:p * north + (t + 1) * SUB, col] - 2.0 * own
                    s_v[l, i, rows_at(t)] = g
                    for kind in range(2):
                        term = w[kind] * g
                        sums[kind][p] = term if t == 0 else sums[kind][p] + term
            for kind in range(2):
                for p in range(PLANES):
                    sg_ref[kind, base + p, :, col] = sums[kind][p]
                my[kind, pl.ds(base, PLANES), col] = stack_rows(
                    [jnp.sum(sums[kind][p], 0, keepdims=True) for p in range(PLANES)])
        for copy in g_stores(c):
            copy.start()
        return carry

    lax.fori_loop(0, chunks, solve, 0)

    for copy in zcopies:
        copy.wait()
    coef = gather(gz, nz, zbuf)
    for m in range(2):
        zpad[m, 0:east] = coef[m]
    for kind in range(2):
        eown[kind] = dot(yw_ref[gy, kind, 0], zpad[0], NT) + dot(yw_ref[gy, kind, 1], zpad[1], NT)
    ecopies = [
        remote(eown.at[kind_to(gy, ny, o)], ebuf.at[o - 1], es.at[o - 1], er.at[o - 1],
               at("gy", lax.rem(gy + o, ny)))
        for o in range(1, ny)
    ]
    for copy in ecopies:
        copy.start()
    ycopies = [
        remote(my.at[kind_to(gy, ny, o)], ybuf.at[o - 1], ys.at[o - 1], yr.at[o - 1],
               at("gy", lax.rem(gy + o, ny)))
        for o in range(1, ny)
    ]
    for copy in ycopies:
        copy.start()

    by = by_ref[gy]
    face = [dot(coef[m], by) for m in range(2)]
    for copy in ecopies:
        copy.wait()
    eleft, eright = gather(gy, ny, ebuf)
    for m in range(2):
        face[m] = face[m] + (
            dot(eleft, yw_ref[gy, 1, m], TN) + dot(eright, yw_ref[gy, 0, m], TN))[0:east]
    for kind in range(2):
        town[kind] = dot(xw_ref[gx, kind, 0], face[0]) + dot(xw_ref[gx, kind, 1], face[1])
    tcopies = [
        remote(town.at[kind_to(gx, nx, o)], tbuf.at[o - 1], ts.at[o - 1], tr.at[o - 1],
               at("gx", lax.rem(gx + o, nx)))
        for o in range(1, nx)
    ]
    for copy in tcopies:
        copy.start()
    bx = bx_ref[gx]
    face = [dot(bx, face[m]) for m in range(2)]

    for copy in xcopies:
        copy.wait()
    px, sx = gather(chip, chips, xbuf)
    first = jnp.where(core == 0, 1.0, 0.0).astype(F32)
    second = 1.0 - first
    xback[0] = px + first * mx[0, mine, :]
    xback[1] = sx + second * mx[1, mine, :]
    back = remote(xback, cx_ref.at[:, mine, :], bs, br, partner)
    back.start()
    cx_ref[0, mine, :] = px + second * xpair[0]
    cx_ref[1, mine, :] = sx + first * xpair[1]
    for copy in rcopies:
        copy.wait()
    rleft, rright = gather(gx, nx, rbuf)
    rright = rright + rown[1]
    back.wait()
    wy = wy_ref[gy]
    cx_ref[0] = dot(by, cx_ref[0]) + dot(wy, rleft, TN)
    cx_ref[1] = dot(by, cx_ref[1] + mx[1]) + dot(wy, rright, TN)

    for copy in tcopies:
        copy.wait()
    tleft, tright = gather(gx, nx, tbuf)
    for m in range(2):
        value = face[m] + dot(xw_ref[gx, 1, m], tleft, TN) + dot(xw_ref[gx, 0, m], tright, TN)
        high = value.astype(BF16).astype(F32)
        cz_ref[:, 3 * m, :] = high
        cz_ref[:, 3 * m + 1, :] = (value - high).astype(BF16).astype(F32)
        cz_ref[:, 3 * m + 2, :] = high
        cz_ref[:, 6 + m, :] = jnp.zeros_like(value)

    for copy in ycopies:
        copy.wait()
    left, right = gather(gy, ny, ybuf)
    cy_ref[0] = left
    cy_ref[1] = right
    for c in range(chunks):
        for copy in g_stores(c):
            copy.wait()


def local_pass(u, s, tables, sizes):
    east, north, upward = u.shape
    nx, ny, nz = sizes
    tiles = upward // LANES
    chunks = east // PLANES
    chips = nx // 2
    half = north // 2
    vmem = pl.BlockSpec(memory_space=pltpu.VMEM)
    smem = pl.BlockSpec(memory_space=pltpu.SMEM)
    hbm = pl.BlockSpec(memory_space=pl.ANY)
    dma = pltpu.SemaphoreType.DMA

    def buf(*dims):
        return pltpu.VMEM(dims, F32)

    names = ("bz", "zmom", "y", "yw", "xw", "wy", "by", "bx")
    return pl.pallas_call(
        functools.partial(local_kernel, sizes, u.shape, tables["factors"]),
        name="local",
        out_shape=(
            jax.ShapeDtypeStruct((tiles, east, north, LANES), F32),
            jax.ShapeDtypeStruct((2, east, SUB, upward), F32),
            jax.ShapeDtypeStruct((east, SUB, north), F32),
            jax.ShapeDtypeStruct((2, east, upward), F32),
            jax.ShapeDtypeStruct((2, north, upward), F32),
        ),
        in_specs=[hbm, hbm] + [vmem] * len(names) + [smem],
        out_specs=(hbm, vmem, vmem, vmem, vmem),
        scratch_shapes=[
            buf(tiles, east + 2, north, LANES),
            buf(tiles, east, north, LANES),
            pltpu.VMEM((east, north, upward), BF16),
            pltpu.VMEM((east, north, upward), BF16),
            buf(2, north, upward), buf(2, east, upward),
            buf(2, north, upward), buf(2, north, upward), buf(2, north, upward),
            buf(2, east, upward), buf(2, east, north),
            buf(nz - 1, east, north), buf(2, LANES, north), buf(ny - 1, east, upward),
            buf(2, half, upward), buf(2, half, upward), buf(chips - 1, half, upward), buf(2, half, upward),
            buf(2, SUB, LANES), buf(ny - 1, SUB, LANES),
            buf(2, SUB, upward), buf(ny - 1, SUB, upward),
            buf(2, SUB, upward), buf(nx - 1, SUB, upward),
            buf(2, SUB, north), buf(nx - 1, SUB, north),
            dma((tiles, chunks)), dma((tiles, chunks)), dma((tiles, chunks)),
            dma((4,)), dma((4,)),
            dma((nz - 1,)), dma((nz - 1,)),
            dma((ny - 1,)), dma((ny - 1,)),
            dma, dma,
            dma((chips - 1,)), dma((chips - 1,)),
            dma, dma,
            dma((ny - 1,)), dma((ny - 1,)),
            dma((ny - 1,)), dma((ny - 1,)),
            dma((nx - 1,)), dma((nx - 1,)),
            dma((nx - 1,)), dma((nx - 1,)),
        ],
        compiler_params=pltpu.CompilerParams(collective_id=0, has_side_effects=True),
    )(u, s, *[tables[name] for name in names], tables["x"])


def final_kernel(
    shape,
    g_ref, u_ref, sg_ref, cz_ref, cy_ref, cx_ref, zadd_ref, ytab_ref, xtab_ref,
    o_ref,
    below_v, g_v, u_v, o_v, gsem, usem, osem,
):
    gx, gy, gz = lax.axis_index("gx"), lax.axis_index("gy"), lax.axis_index("gz")
    east, north, upward = shape
    tiles = upward // LANES
    steps = north // SUB
    chunks = east // PLANES

    def lanes(l):
        return pl.ds(l * LANES, LANES)

    def loads(c):
        out = []
        rows = pl.ds(c * PLANES, PLANES)
        for l in range(tiles):
            out.append(pltpu.make_async_copy(g_ref.at[l, rows], g_v.at[l, rows], gsem.at[l, c]))
            out.append(pltpu.make_async_copy(
                u_ref.at[rows, :, lanes(l)], u_v.at[l, rows], usem.at[l, c]))
        return out

    def stores(c):
        rows = pl.ds(c * PLANES, PLANES)
        return [
            pltpu.make_async_copy(o_v.at[l, rows], o_ref.at[rows, :, lanes(l)], osem.at[l, c])
            for l in range(tiles)
        ]

    for c in range(chunks):
        for copy in loads(c):
            copy.start()

    below_v[...] = cx_ref[...]
    zadd = zadd_ref[gz]
    sub = lax.broadcasted_iota(jnp.int32, (SUB, LANES), 0)

    def scan(value, backward):
        def shifted(x, d):
            if backward:
                return jnp.where(sub < SUB - d, pltpu.roll(x, SUB - d, 0), 0.0)
            return jnp.where(sub >= d, pltpu.roll(x, d, 0), 0.0)

        for d in (1, 2, 4):
            value = value + shifted(value, d)
        return shifted(value, 1)

    def step(c, carry):
        for copy in loads(c):
            copy.wait()
        base = pl.multiple_of(c * PLANES, PLANES)
        wx = [[xtab_ref[kind, gx * east + base + p] for p in range(PLANES)] for kind in range(2)]
        add = []
        for p in range(PLANES):
            cz = cz_ref[base + p].T.astype(BF16)
            add.append(jnp.dot(cz, zadd, preferred_element_type=F32))
        for l in range(tiles):
            col = slice(l * LANES, (l + 1) * LANES)
            edge = [cy_ref[kind, pl.ds(base, PLANES), col] for kind in range(2)]
            low, high = [], []
            for p in range(PLANES):
                su, sv = sg_ref[0, base + p, :, col], sg_ref[1, base + p, :, col]
                low.append(scan(su, False) + edge[0][p:p + 1])
                high.append(scan(sv, True) + edge[1][p:p + 1] + sv)
            for t in range(steps):
                row = slice(t * SUB, (t + 1) * SUB)
                wu, wv = ytab_ref[gy, 0, row], ytab_ref[gy, 1, row]
                below, above = below_v[0, row, col], below_v[1, row, col]
                for p in range(PLANES):
                    i = base + p
                    g = g_v[l, i, row]
                    low[p] = low[p] + wu * g
                    high[p] = high[p] - wv * g
                    h = wv * low[p] + wu * high[p]
                    below = below + wx[0][p] * h
                    above = above - wx[1][p] * h
                    own = u_v[l, i, pl.ds(t, SUB, stride=steps), :]
                    o_v[l, i, pl.ds(t, SUB, stride=steps), :] = (
                        own + add[p][row, col] + (wx[1][p] * below + wx[0][p] * above))
                below_v[0, row, col] = below
                below_v[1, row, col] = above
        for copy in stores(c):
            copy.start()
        return carry

    lax.fori_loop(0, chunks, step, 0)
    for c in range(chunks):
        for copy in stores(c):
            copy.wait()


def final_pass(g, u, sg, cz, cy, cx, tables):
    east, north, upward = u.shape
    tiles = upward // LANES
    chunks = east // PLANES
    vmem = pl.BlockSpec(memory_space=pltpu.VMEM)
    smem = pl.BlockSpec(memory_space=pltpu.SMEM)
    hbm = pl.BlockSpec(memory_space=pl.ANY)
    block = pltpu.VMEM((tiles, east, north, LANES), F32)
    return pl.pallas_call(
        functools.partial(final_kernel, u.shape),
        name="final",
        out_shape=jax.ShapeDtypeStruct(u.shape, F32),
        in_specs=[hbm, hbm, vmem, vmem, vmem, vmem, vmem, vmem, smem],
        out_specs=hbm,
        scratch_shapes=[
            pltpu.VMEM((2, north, upward), F32),
            block, block, block,
            pltpu.SemaphoreType.DMA((tiles, chunks)),
            pltpu.SemaphoreType.DMA((tiles, chunks)),
            pltpu.SemaphoreType.DMA((tiles, chunks)),
        ],
    )(g, u, sg, cz, cy, cx, tables["zadd"], tables["y"], tables["x"])


def local(sizes, u, s):
    tables = make_tables(u.shape, sizes)
    g, sg, cz, cy, cx = local_pass(u, s, tables, sizes)
    return final_pass(g, u, sg, cz, cy, cx, tables)


def solution(mesh):
    sizes = tuple(mesh.shape[name] for name in ("gx", "gy", "gz"))
    spec = P("gx", "gy", "gz")
    return jax.shard_map(
        functools.partial(local, sizes), mesh=mesh, in_specs=(spec, spec), out_specs=spec, check_vma=False
    )
```

time: 66.7 us -> 56.8 us (0.85)
  Pallas kernels: 66.5 us -> 56.6 us
    pallas_call x3 -> x1, Pallas kernels: 46.3 us -> 13 us  [final_pass(): pl.pallas_call(functools.partial(final_kernel, u.shape), name='final', ou...]
    pallas_call x1, Pallas kernels: 20.2 us -> 43.6 us  [local_pass(): pl.pallas_call(functools.partial(local_kernel, sizes, u.shape, tables['fa...]
where the time goes in v1:
time: 56.8 us; the launch traced here: 56.6 us
  Pallas kernels  56.6 us (100%)
    pallas_call x1, Pallas kernels, local_pass(): pl.pallas_call(functools.partial(local_kernel, sizes, u.shape, tables['fa...  43.6 us
    pallas_call x1, Pallas kernels, final_pass(): pl.pallas_call(functools.partial(final_kernel, u.shape), name='final', ou...  13 us

profile of v1, /device:TPU:1, one launch (start us, length us, event | category | flops | bytes accessed | tf_op | source)
XLA Modules:
  0.0 56.6 jit_solution(7157987690574995544)
XLA Ops:
  0.0 43.6 %local.1 = (f32[2,64,128,128]{3,2,1,0:T(8,128)}, f32[2,64,8,256]{3,2,1,0:T(8,128)}, f32[64,8,128]{2,1,0:T(8,128)}, f32[2,64,256]{2,1,0:T(8,128)}, f32[2,128,256]{2,1,0:T(8,128)}) custom-call(f32[64,128,256]{2,1,0:T(8,128)} %u_ref.3, f32[64,128,256]{2,1,0:T(8,128)} %s_ref.1, bf16[4,2,256,256]{3,2,1,0:T(8,128)(2,1)} %constant.20.clone.bz_ref, ...), custom_call_target="tpu_custom_call" | custom-call | tf_op jit(solution)/shard_map/local/pallas_call | solution.py:506
  43.6 13.0 %final.1 = f32[64,128,256]{2,1,0:T(8,128)} custom-call(f32[2,64,128,128]{3,2,1,0:T(8,128)} %get-tuple-element.10.g_ref, f32[64,128,256]{2,1,0:T(8,128)} %u_ref.3, f32[2,64,8,256]{3,2,1,0:T(8,128)} %get-tuple-element.11.sg_ref, f32[64,8,128]{2,1,0:T(8,128)} %get-tuple-element.12.cz_ref, f32[2,64,256]{2,1,0:T(8,128)} %get-tuple-element.13.cy_ref, ...), custom_call_target="tpu_custom_call" | custom-call | tf_op jit(solution)/shard_map/final/pallas_call | solution.py:649

commit v2 on v1

v2 whole, which is shorter than its diff:
```python
import functools

import jax
import jax.numpy as jnp
import numpy as np
from jax import lax
from jax.experimental import pallas as pl
from jax.experimental.pallas import tpu as pltpu
from jax.sharding import PartitionSpec as P

MESH = pl.DeviceIdType.MESH
HIGH = lax.Precision.HIGHEST
F32 = jnp.float32
BF16 = jnp.bfloat16
LANES = 128
SUB = 8


def generators(whole, factor):
    half = 0.5 * factor
    theta = np.arccosh(1.0 + 0.5 / half)
    scale = np.sqrt(1.0 / (half * np.sinh(theta) * np.sinh((whole + 1) * theta)))
    index = np.arange(whole, dtype=np.float64)
    return np.sinh((index + 1) * theta) * scale, np.sinh((whole - index) * theta) * scale


def diagonal_blocks(u, v, members):
    extent = u.shape[0] // members
    blocks = []
    for member in range(members):
        part = slice(member * extent, (member + 1) * extent)
        own_u, own_v = u[part], v[part]
        lower = np.outer(own_v, own_u)
        blocks.append(np.where(np.tri(extent, dtype=bool), lower, lower.T))
    return np.stack(blocks)


def split_bf16(values):
    high = values.astype(np.float32).astype(BF16)
    low = (values - high.astype(np.float64)).astype(np.float32).astype(BF16)
    return np.asarray(high), np.asarray(low)


def split(values):
    high = values.astype(BF16)
    return high, (values - high.astype(F32)).astype(BF16)


def make_tables(shape, members):
    east, north, upward = shape
    wholes = [extent * count for extent, count in zip(shape, members)]
    factors = [float(whole * whole // 4) for whole in wholes]
    order = np.arange(north)
    order = (north // SUB) * (order % SUB) + order // SUB

    ux, vx = generators(wholes[0], factors[0])
    uy, vy = generators(wholes[1], factors[1])
    uz, vz = generators(wholes[2], factors[2])
    tables = {"factors": factors}
    tables["x"] = np.stack([ux, vx]).astype(np.float32)

    own = np.stack([w.reshape(members[1], north)[:, order] for w in (uy, vy)], 1)
    tables["y"] = np.repeat(own[..., None], LANES, -1).astype(np.float32)
    by = diagonal_blocks(uy, vy, members[1])[:, order][:, :, order]
    tables["by"] = by.astype(np.float32)
    tables["bx"] = diagonal_blocks(ux, vx, members[0]).astype(np.float32)
    yw = np.zeros((members[1], 2, 2, SUB, north), np.float32)
    xw = np.zeros((members[0], 2, 2, SUB, east), np.float32)
    for slot in range(2):
        yw[:, :, slot, slot] = own
        for kind, w in enumerate((ux, vx)):
            xw[:, kind, slot, slot] = w.reshape(members[0], east)
    tables["yw"], tables["xw"] = yw, xw
    wy = np.zeros((members[1], SUB, north), np.float32)
    wy[:, 0] = own[:, 1]
    wy[:, 1] = own[:, 0]
    tables["wy"] = wy

    bzh, bzl = split_bf16(diagonal_blocks(uz, vz, members[2]))
    tables["bz"] = np.stack([bzh, bzl], 1)
    zu, zv = uz.reshape(members[2], upward), vz.reshape(members[2], upward)
    uh, ul = split_bf16(zu)
    vh, vl = split_bf16(zv)
    zero = np.zeros_like(uh)
    tables["zmom"] = np.stack([uh, ul, vh, vl] + [zero] * 12, 1)
    tables["zadd"] = np.stack([vh, vh, vl, uh, uh, ul, zero, zero], 1)
    return tables


def at(axis, index):
    return {axis: index}


def greet(partners):
    barrier = pltpu.get_barrier_semaphore()
    for partner in partners:
        pl.semaphore_signal(barrier, inc=1, device_id=partner, device_id_type=MESH)
    pl.semaphore_wait(barrier, len(partners))


def remote(src, dst, send, recv, partner):
    return pltpu.make_async_remote_copy(
        src_ref=src, dst_ref=dst, send_sem=send, recv_sem=recv, device_id=partner, device_id_type=MESH
    )


def kind_to(me, count, o):
    return jnp.where(lax.rem(me + o, count) > me, 0, 1)


def gather(me, count, buf):
    left = right = None
    for o in range(1, count):
        low = jnp.where(lax.rem(me + count - o, count) < me, 1.0, 0.0).astype(F32)
        piece = buf[o - 1]
        left = piece * low if left is None else left + piece * low
        right = piece * (1.0 - low) if right is None else right + piece * (1.0 - low)
    return left, right


NN = (((1,), (0,)), ((), ()))
NT = (((1,), (1,)), ((), ()))
TN = (((0,), (0,)), ((), ()))


def dot(a, b, dims=NN):
    if dims == TN:
        return lax.dot_general(a, b, dims, precision=HIGH, preferred_element_type=F32)
    ah, al = split(a)
    bh, bl = split(b)
    left = jnp.concatenate([ah, al, ah], 1)
    right = jnp.concatenate([bl, bh, bh], dims[0][1][0])
    return lax.dot_general(left, right, dims, preferred_element_type=F32)


PLANES = 8
LOAD = 16


def stack_rows(rows, width=LANES):
    sub = lax.broadcasted_iota(jnp.int32, (SUB, width), 0)
    out = jnp.zeros((SUB, width), F32)
    for p, row in enumerate(rows):
        out = jnp.where(sub == p, row, out)
    return out


def local_kernel(
    sizes, shape, factors,
    u_ref, s_ref, bz_hbm, zmom_hbm, ytab_hbm, yw_hbm, xw_hbm, wy_hbm, by_hbm, bx_hbm, zadd_hbm, xtab_ref,
    g_v, u_v, sg_ref, cz_ref, cy_ref, cx_ref, ytab_ref, zadd_ref,
    bz_ref, zmom_ref, yw_ref, xw_ref, wy_ref, by_ref, bx_ref, tsem,
    s_v, fh0, fl0, fh1, fl1, y0, y1, hy, mxf, mxu, mx, my, mz,
    zbuf, zpad, ybuf, xpair, xtot, xbuf, xback, eown, ebuf, qown, qbuf, rown, rbuf, town, tbuf,
    usem, ssem, hs, hr, zs, zr, ys, yr, ps, pr, xs, xr, bs, br, es, er, qs, qr, rs, rr, ts, tr,
):
    gx, gy, gz = lax.axis_index("gx"), lax.axis_index("gy"), lax.axis_index("gz")
    nx, ny, nz = sizes
    east, north, upward = shape
    tiles = upward // LANES
    steps = north // SUB
    chunks = east // PLANES
    pairs = chunks // 2
    blocks = east // LOAD
    rx, ry, _ = factors
    chips = nx // 2
    half = north // 2
    chip, core = gx // 2, lax.rem(gx, 2)
    mine = pl.ds(pl.multiple_of(core * half, half), half)
    theirs = pl.ds(pl.multiple_of((1 - core) * half, half), half)
    partner = at("gx", chip * 2 + 1 - core)

    def u_loads(b):
        rows = pl.ds(b * LOAD, LOAD)
        return [
            pltpu.make_async_copy(
                u_ref.at[rows, pl.ds(k * steps, steps), :], u_v.at[pl.ds(1 + b * LOAD, LOAD), :, k, :],
                usem.at[b, k])
            for k in range(SUB)
        ]

    def s_loads(b):
        rows = pl.ds(b * LOAD, LOAD)
        return [
            pltpu.make_async_copy(
                s_ref.at[rows, pl.ds(k * steps, steps), :], s_v.at[rows, :, k, :], ssem.at[b, k])
            for k in range(SUB)
        ]

    early = sorted({0, blocks - 1})
    for b in early + [b for b in range(blocks) if b not in early]:
        for copy in u_loads(b):
            copy.start()
    for b in range(blocks):
        for copy in s_loads(b):
            copy.start()

    table_loads = [
        pltpu.make_async_copy(hbm.at[index], ref, tsem.at[n])
        for n, (hbm, index, ref) in enumerate((
            (bz_hbm, gz, bz_ref), (zmom_hbm, gz, zmom_ref), (ytab_hbm, gy, ytab_ref), (yw_hbm, gy, yw_ref),
            (xw_hbm, gx, xw_ref), (wy_hbm, gy, wy_ref), (by_hbm, gy, by_ref), (bx_hbm, gx, bx_ref),
            (zadd_hbm, gz, zadd_ref)))
    ]
    for copy in table_loads:
        copy.start()

    def ring(axis, me, count):
        return [at(axis, lax.rem(me + o, count)) for o in range(1, count)]

    greet(ring("gx", gx, nx) + ring("gy", gy, ny) + ring("gz", gz, nz))

    xr_, xl_ = lax.rem(gx + 1, nx), lax.rem(gx + nx - 1, nx)
    yr_, yl_ = lax.rem(gy + 1, ny), lax.rem(gy + ny - 1, ny)
    halos = [
        remote(u_ref.at[:, north - 1, :], hy.at[0], hs.at[2], hr.at[2], at("gy", yr_)),
        remote(u_ref.at[:, 0, :], hy.at[1], hs.at[3], hr.at[3], at("gy", yl_)),
        remote(u_v.at[east], u_v.at[0], hs.at[0], hr.at[0], at("gx", xr_)),
        remote(u_v.at[1], u_v.at[east + 1], hs.at[1], hr.at[1], at("gx", xl_)),
    ]
    for copy in halos[:2]:
        copy.start()
    for b in early:
        for copy in u_loads(b):
            copy.wait()
    for copy in halos[2:]:
        copy.start()

    sub = lax.broadcasted_iota(jnp.int32, (SUB, LANES), 0)

    def cols(l):
        return slice(l * LANES, (l + 1) * LANES)

    def rows_at(t):
        return slice(t * SUB, (t + 1) * SUB)

    mxu[...] = jnp.zeros_like(mxu)
    mxf[...] = jnp.zeros_like(mxf)
    zpad[...] = jnp.zeros_like(zpad)

    def weights(base):
        return [[xtab_ref[kind, gx * east + base + p] for p in range(PLANES)] for kind in range(2)]

    def pre(c, carry):
        block = c * PLANES // LOAD
        waits = lax.rem(c * PLANES, LOAD) == 0
        for b in early:
            waits = jnp.logical_and(waits, block != b)

        @pl.when(waits)
        def _():
            for copy in u_loads(block):
                copy.wait()

        base = c * PLANES
        w = weights(base)
        for l in range(tiles):
            for t in range(steps):
                acc = [mxu[kind, rows_at(t), cols(l)] for kind in range(2)]
                for p in range(PLANES):
                    own = u_v[base + p + 1, t, :, cols(l)]
                    for kind in range(2):
                        acc[kind] = acc[kind] + w[kind][p] * own
                for kind in range(2):
                    mxu[kind, rows_at(t), cols(l)] = acc[kind]
        return carry

    lax.fori_loop(0, chunks, pre, 0)

    for copy in halos:
        copy.wait()
    before = jnp.where(gx > 0, 1.0, 0.0).astype(F32)
    after = jnp.where(gx < nx - 1, 1.0, 0.0).astype(F32)
    south = jnp.where(gy > 0, 1.0, 0.0).astype(F32)
    nord = jnp.where(gy < ny - 1, 1.0, 0.0).astype(F32)
    u_v[0] = u_v[0] * before
    u_v[east + 1] = u_v[east + 1] * after

    for copy in table_loads:
        copy.wait()
    zmom = zmom_ref[...]
    halves = ((fh0, fl0), (fh1, fl1))

    def z_moments(source, k, c):
        mom = None
        for f in source:
            flat = f[k].reshape(PLANES * north, upward)
            part = lax.dot_general(zmom, flat, NT, preferred_element_type=F32)
            mom = part if mom is None else mom + part
        for kind in range(2):
            m = mom[2 * kind:2 * kind + 1] + mom[2 * kind + 1:2 * kind + 2]
            mz[kind, pl.ds(pl.multiple_of(c * PLANES, PLANES), PLANES), :] = stack_rows(
                [m[:, p * north:(p + 1) * north] for p in range(PLANES)])

    def rhs(target, k, c):
        high_ref, low_ref = target
        base = pl.multiple_of(c * PLANES, PLANES)
        w = weights(base)
        for l in range(tiles):
            col = cols(l)
            edge = [hy[0, pl.ds(base, PLANES), col] * south, hy[1, pl.ds(base, PLANES), col] * nord]
            for t2 in range(0, steps, 2):
                acc = [[mxf[kind, rows_at(t2 + j), col] for j in range(2)] for kind in range(2)]
                column = [[u_v[base + p, t2 + j, :, col] for p in range(PLANES + 2)] for j in range(2)]
                for p in range(PLANES):
                    i = base + p
                    if t2 == 0:
                        below = pltpu.roll(u_v[i + 1, steps - 1, :, col], 1, 0)
                        below = jnp.where(sub == 0, edge[0][p:p + 1], below)
                    else:
                        below = u_v[i + 1, t2 - 1, :, col]
                    if t2 == steps - 2:
                        above = pltpu.roll(u_v[i + 1, 0, :, col], SUB - 1, 0)
                        above = jnp.where(sub == SUB - 1, edge[1][p:p + 1], above)
                    else:
                        above = u_v[i + 1, t2 + 2, :, col]
                    out = []
                    for j in range(2):
                        own = column[j][p + 1]
                        across = column[j][p] + column[j][p + 2]
                        along = (below + column[1][p + 1]) if j == 0 else (column[0][p + 1] + above)
                        if rx == ry:
                            spread = rx * ((across + along) + (2.0 / rx - 4.0) * own)
                        else:
                            spread = rx * across + ry * along + (2.0 - 2.0 * rx - 2.0 * ry) * own
                        f = s_v[i, t2 + j, :, col] + spread
                        for kind in range(2):
                            acc[kind][j] = acc[kind][j] + w[kind][p] * f
                        out.append(f)
                    pair = jnp.concatenate(out, 0)
                    high = pair.astype(BF16)
                    rows = slice(t2 * SUB, (t2 + 2) * SUB)
                    high_ref[k, p, rows, col] = high
                    low_ref[k, p, rows, col] = (pair - high.astype(F32)).astype(BF16)
                for kind in range(2):
                    for j in range(2):
                        mxf[kind, rows_at(t2 + j), col] = acc[kind][j]

    def rhs_pair(k, carry):
        waits = lax.rem(k * 2 * PLANES, LOAD) == 0

        @pl.when(waits)
        def _():
            for copy in s_loads(k * 2 * PLANES // LOAD):
                copy.wait()

        late = jnp.maximum(k - 1, 0)
        z_moments(halves[1], late, 2 * late + 1)
        rhs(halves[0], k, 2 * k)
        z_moments(halves[0], k, 2 * k)
        rhs(halves[1], k, 2 * k + 1)
        return carry

    lax.fori_loop(0, pairs, rhs_pair, 0)
    z_moments(halves[1], pairs - 1, chunks - 1)

    zcopies = [
        remote(mz.at[kind_to(gz, nz, o)], zbuf.at[o - 1], zs.at[o - 1], zr.at[o - 1],
               at("gz", lax.rem(gz + o, nz)))
        for o in range(1, nz)
    ]
    for copy in zcopies:
        copy.start()

    def solve_up(high, low):
        stack = jnp.concatenate([bz_ref[1], bz_ref[0], bz_ref[0]], 0)
        return jnp.dot(jnp.concatenate([high, low, high], 1), stack, preferred_element_type=F32)

    fold_h, fold_l = split(mxf[...].reshape(2 * north, upward))
    mx[...] = solve_up(fold_h, fold_l).reshape(2, north, upward) - 2.0 * mxu[...]

    pair = remote(mx.at[:, theirs, :], xpair, ps, pr, partner)
    pair.start()
    for kind in range(2):
        qown[kind] = dot(yw_ref[kind, 0], mx[0]) + dot(yw_ref[kind, 1], mx[1])
    qcopies = [
        remote(qown.at[kind_to(gy, ny, o)], qbuf.at[o - 1], qs.at[o - 1], qr.at[o - 1],
               at("gy", lax.rem(gy + o, ny)))
        for o in range(1, ny)
    ]
    for copy in qcopies:
        copy.start()
    xcopies = [
        remote(xtot.at[kind_to(chip, chips, o)], xbuf.at[o - 1], xs.at[o - 1], xr.at[o - 1],
               at("gx", lax.rem(chip + o, chips) * 2 + core))
        for o in range(1, chips)
    ]
    rcopies = [
        remote(rown.at[kind_to(gx, nx, o)], rbuf.at[o - 1], rs.at[o - 1], rr.at[o - 1],
               at("gx", lax.rem(gx + o, nx)))
        for o in range(1, nx)
    ]

    def send_chips():
        pair.wait()
        xtot[0] = mx[0, mine, :] + xpair[0]
        xtot[1] = mx[1, mine, :] + xpair[1]
        for copy in xcopies:
            copy.start()

    def send_edges():
        for copy in qcopies:
            copy.wait()
        qleft, qright = gather(gy, ny, qbuf)
        for kind in range(2):
            rown[kind] = stack_rows([qleft[kind:kind + 1], qright[kind:kind + 1]], upward)
        for copy in rcopies:
            copy.start()

    def multiply(source, k, target):
        high_ref, low_ref = source
        target[...] = solve_up(
            high_ref[k].reshape(PLANES * north, upward), low_ref[k].reshape(PLANES * north, upward))

    def finish(source, c):
        base = pl.multiple_of(c * PLANES, PLANES)
        for l in range(tiles):
            col = cols(l)
            sums = [[None] * PLANES for _ in range(2)]
            for t in range(steps):
                w = [ytab_ref[kind, rows_at(t)] for kind in range(2)]
                for p in range(PLANES):
                    i = base + p
                    own = u_v[i + 1, t, :, col]
                    g = source[p * north + t * SUB:p * north + (t + 1) * SUB, col] - 2.0 * own
                    g_v[i, t, :, col] = g
                    for kind in range(2):
                        term = w[kind] * g
                        sums[kind][p] = term if t == 0 else sums[kind][p] + term
            for kind in range(2):
                for p in range(PLANES):
                    sg_ref[kind, base + p, :, col] = sums[kind][p]
                my[kind, pl.ds(base, PLANES), col] = stack_rows(
                    [jnp.sum(sums[kind][p], 0, keepdims=True) for p in range(PLANES)])

    def solve_pair(k, carry):
        @pl.when(k == min(1, pairs - 1))
        def _():
            send_chips()

        @pl.when(k == pairs - 1)
        def _():
            send_edges()

        multiply(halves[0], k, y0)
        finish(y1, jnp.maximum(2 * k - 1, 0))
        multiply(halves[1], k, y1)
        finish(y0, 2 * k)
        return carry

    lax.fori_loop(0, pairs, solve_pair, 0)
    finish(y1, chunks - 1)

    for copy in zcopies:
        copy.wait()
    coef = gather(gz, nz, zbuf)
    for m in range(2):
        zpad[m, 0:east] = coef[m]
    for kind in range(2):
        eown[kind] = dot(yw_ref[kind, 0], zpad[0], NT) + dot(yw_ref[kind, 1], zpad[1], NT)
    ecopies = [
        remote(eown.at[kind_to(gy, ny, o)], ebuf.at[o - 1], es.at[o - 1], er.at[o - 1],
               at("gy", lax.rem(gy + o, ny)))
        for o in range(1, ny)
    ]
    for copy in ecopies:
        copy.start()
    ycopies = [
        remote(my.at[kind_to(gy, ny, o)], ybuf.at[o - 1], ys.at[o - 1], yr.at[o - 1],
               at("gy", lax.rem(gy + o, ny)))
        for o in range(1, ny)
    ]
    for copy in ycopies:
        copy.start()

    by = by_ref[...]
    face = [dot(coef[m], by) for m in range(2)]
    for copy in ecopies:
        copy.wait()
    eleft, eright = gather(gy, ny, ebuf)
    for m in range(2):
        face[m] = face[m] + (
            dot(eleft, yw_ref[1, m], TN) + dot(eright, yw_ref[0, m], TN))[0:east]
    for kind in range(2):
        town[kind] = dot(xw_ref[kind, 0], face[0]) + dot(xw_ref[kind, 1], face[1])
    tcopies = [
        remote(town.at[kind_to(gx, nx, o)], tbuf.at[o - 1], ts.at[o - 1], tr.at[o - 1],
               at("gx", lax.rem(gx + o, nx)))
        for o in range(1, nx)
    ]
    for copy in tcopies:
        copy.start()
    bx = bx_ref[...]
    face = [dot(bx, face[m]) for m in range(2)]

    for copy in xcopies:
        copy.wait()
    px, sx = gather(chip, chips, xbuf)
    first = jnp.where(core == 0, 1.0, 0.0).astype(F32)
    second = 1.0 - first
    xback[0] = px + first * mx[0, mine, :]
    xback[1] = sx + second * mx[1, mine, :]
    back = remote(xback, cx_ref.at[:, mine, :], bs, br, partner)
    back.start()
    cx_ref[0, mine, :] = px + second * xpair[0]
    cx_ref[1, mine, :] = sx + first * xpair[1]
    for copy in rcopies:
        copy.wait()
    rleft, rright = gather(gx, nx, rbuf)
    rright = rright + rown[1]
    back.wait()
    wy = wy_ref[...]
    cx_ref[0] = dot(by, cx_ref[0]) + dot(wy, rleft, TN)
    cx_ref[1] = dot(by, cx_ref[1] + mx[1]) + dot(wy, rright, TN)

    for copy in tcopies:
        copy.wait()
    tleft, tright = gather(gx, nx, tbuf)
    for m in range(2):
        value = face[m] + dot(xw_ref[1, m], tleft, TN) + dot(xw_ref[0, m], tright, TN)
        high = value.astype(BF16).astype(F32)
        cz_ref[:, 3 * m, :] = high
        cz_ref[:, 3 * m + 1, :] = (value - high).astype(BF16).astype(F32)
        cz_ref[:, 3 * m + 2, :] = high
        cz_ref[:, 6 + m, :] = jnp.zeros_like(value)

    for copy in ycopies:
        copy.wait()
    left, right = gather(gy, ny, ybuf)
    cy_ref[0] = left
    cy_ref[1] = right


def local_pass(u, s, tables, sizes):
    east, north, upward = u.shape
    nx, ny, nz = sizes
    steps = north // SUB
    pairs = east // (2 * PLANES)
    blocks = east // LOAD
    chips = nx // 2
    half = north // 2
    vmem = pl.BlockSpec(memory_space=pltpu.VMEM)
    smem = pl.BlockSpec(memory_space=pltpu.SMEM)
    hbm = pl.BlockSpec(memory_space=pltpu.HBM)
    dma = pltpu.SemaphoreType.DMA

    def buf(*dims):
        return pltpu.VMEM(dims, F32)

    def halves():
        return pltpu.VMEM((pairs, PLANES, north, upward), BF16)

    names = ("bz", "zmom", "y", "yw", "xw", "wy", "by", "bx", "zadd")
    return pl.pallas_call(
        functools.partial(local_kernel, sizes, u.shape, tables["factors"]),
        name="local",
        out_shape=(
            buf(east, steps, SUB, upward),
            buf(east + 2, steps, SUB, upward),
            buf(2, east, SUB, upward),
            buf(east, SUB, north),
            buf(2, east, upward),
            buf(2, north, upward),
            buf(2, north, LANES),
            pltpu.VMEM((SUB, upward), BF16),
        ),
        in_specs=[hbm, hbm] + [hbm] * len(names) + [smem],
        out_specs=(vmem,) * 8,
        scratch_shapes=[
            pltpu.VMEM((2, upward, upward), BF16), pltpu.VMEM((16, upward), BF16),
            buf(2, 2, SUB, north), buf(2, 2, SUB, east), buf(SUB, north), buf(north, north), buf(east, east),
            dma((len(names),)),
            buf(east, steps, SUB, upward),
            halves(), halves(), halves(), halves(),
            buf(PLANES * north, upward), buf(PLANES * north, upward),
            buf(2, east, upward),
            buf(2, north, upward), buf(2, north, upward), buf(2, north, upward),
            buf(2, east, upward), buf(2, east, north),
            buf(nz - 1, east, north), buf(2, LANES, north), buf(ny - 1, east, upward),
            buf(2, half, upward), buf(2, half, upward), buf(chips - 1, half, upward), buf(2, half, upward),
            buf(2, SUB, LANES), buf(ny - 1, SUB, LANES),
            buf(2, SUB, upward), buf(ny - 1, SUB, upward),
            buf(2, SUB, upward), buf(nx - 1, SUB, upward),
            buf(2, SUB, north), buf(nx - 1, SUB, north),
            dma((blocks, SUB)), dma((blocks, SUB)),
            dma((4,)), dma((4,)),
            dma((nz - 1,)), dma((nz - 1,)),
            dma((ny - 1,)), dma((ny - 1,)),
            dma, dma,
            dma((chips - 1,)), dma((chips - 1,)),
            dma, dma,
            dma((ny - 1,)), dma((ny - 1,)),
            dma((ny - 1,)), dma((ny - 1,)),
            dma((nx - 1,)), dma((nx - 1,)),
            dma((nx - 1,)), dma((nx - 1,)),
        ],
        compiler_params=pltpu.CompilerParams(
            collective_id=0, has_side_effects=True, vmem_limit_bytes=LOCAL_VMEM),
    )(*[pltpu.with_memory_space_constraint(a, pltpu.HBM) for a in [u, s] + [tables[name] for name in names + ("x",)]])


LOCAL_VMEM = 34 * 2**20
FINAL_VMEM = 24 * 2**20


def final_kernel(
    shape,
    g_v, u_v, sg_ref, cz_ref, cy_ref, cx_ref, zadd_ref, ytab_ref, xtab_ref,
    o_ref,
    edge_v, o_v, osem,
):
    gx, gy, gz = lax.axis_index("gx"), lax.axis_index("gy"), lax.axis_index("gz")
    east, north, upward = shape
    tiles = upward // LANES
    steps = north // SUB
    chunks = east // PLANES

    def stores(c):
        rows = pl.ds(c * PLANES, PLANES)
        return [
            pltpu.make_async_copy(
                o_v.at[rows, :, k, :], o_ref.at[rows, pl.ds(k * steps, steps), :], osem.at[c, k])
            for k in range(SUB)
        ]

    edge_v[...] = cx_ref[...]
    zadd = zadd_ref[...]
    sub = lax.broadcasted_iota(jnp.int32, (SUB, LANES), 0)

    def scan(value, backward):
        def shifted(x, d):
            if backward:
                return jnp.where(sub < SUB - d, pltpu.roll(x, SUB - d, 0), 0.0)
            return jnp.where(sub >= d, pltpu.roll(x, d, 0), 0.0)

        for d in (1, 2, 4):
            value = value + shifted(value, d)
        return shifted(value, 1)

    def step(c, carry):
        base = pl.multiple_of(c * PLANES, PLANES)
        wx = [[xtab_ref[kind, gx * east + base + p] for p in range(PLANES)] for kind in range(2)]
        add = []
        for p in range(PLANES):
            cz = cz_ref[base + p].T.astype(BF16)
            add.append(jnp.dot(cz, zadd, preferred_element_type=F32))
        for l in range(tiles):
            col = slice(l * LANES, (l + 1) * LANES)
            edge = [cy_ref[kind, pl.ds(base, PLANES), col] for kind in range(2)]
            low, high = [], []
            for p in range(PLANES):
                su, sv = sg_ref[0, base + p, :, col], sg_ref[1, base + p, :, col]
                low.append(scan(su, False) + edge[0][p:p + 1])
                high.append(scan(sv, True) + edge[1][p:p + 1] + sv)
            for t in range(steps):
                row = slice(t * SUB, (t + 1) * SUB)
                wu, wv = ytab_ref[0, row], ytab_ref[1, row]
                below, above = edge_v[0, row, col], edge_v[1, row, col]
                for p in range(PLANES):
                    i = base + p
                    g = g_v[i, t, :, col]
                    low[p] = low[p] + wu * g
                    high[p] = high[p] - wv * g
                    h = wv * low[p] + wu * high[p]
                    below = below + wx[0][p] * h
                    above = above - wx[1][p] * h
                    o_v[i, t, :, col] = (
                        u_v[i + 1, t, :, col] + add[p][row, col] + (wx[1][p] * below + wx[0][p] * above))
                edge_v[0, row, col] = below
                edge_v[1, row, col] = above
        for copy in stores(c):
            copy.start()
        return carry

    lax.fori_loop(0, chunks, step, 0)
    for c in range(chunks):
        for copy in stores(c):
            copy.wait()


def final_pass(g, u, sg, cz, cy, cx, ytab, zadd, tables, shape):
    east, north, upward = shape
    steps = north // SUB
    chunks = east // PLANES
    vmem = pl.BlockSpec(memory_space=pltpu.VMEM)
    smem = pl.BlockSpec(memory_space=pltpu.SMEM)
    return pl.pallas_call(
        functools.partial(final_kernel, shape),
        name="final",
        out_shape=jax.ShapeDtypeStruct(shape, F32),
        in_specs=[vmem] * 8 + [smem],
        out_specs=pl.BlockSpec(memory_space=pl.ANY),
        scratch_shapes=[
            pltpu.VMEM((2, north, upward), F32),
            pltpu.VMEM((east, steps, SUB, upward), F32),
            pltpu.SemaphoreType.DMA((chunks, SUB)),
        ],
        compiler_params=pltpu.CompilerParams(vmem_limit_bytes=FINAL_VMEM),
    )(g, u, sg, cz, cy, cx, zadd, ytab, tables["x"])


def local(sizes, u, s):
    tables = make_tables(u.shape, sizes)
    g, padded, *faces = local_pass(u, s, tables, sizes)
    return final_pass(g, padded, *faces, tables, u.shape)


def solution(mesh):
    sizes = tuple(mesh.shape[name] for name in ("gx", "gy", "gz"))
    spec = P("gx", "gy", "gz")
    return jax.shard_map(
        functools.partial(local, sizes), mesh=mesh, in_specs=(spec, spec), out_specs=spec, check_vma=False
    )
```

time: 56.8 us -> 45.2 us (0.80)
  Pallas kernels: 56.6 us -> 45.1 us
    pallas_call x1, Pallas kernels: 43.6 us -> 36.1 us  [local_pass(): pl.pallas_call(functools.partial(local_kernel, sizes, u.shape, tables['fa...]
    pallas_call x1, Pallas kernels: 13 us -> 8.94 us  [final_pass(): pl.pallas_call(functools.partial(final_kernel, shape), name='final', out_...]
where the time goes in v2:
time: 45.2 us; the launch traced here: 45.1 us
  Pallas kernels  45.1 us (100%)
    pallas_call x1, Pallas kernels, local_pass(): pl.pallas_call(functools.partial(local_kernel, sizes, u.shape, tables['fa...  36.1 us
    pallas_call x1, Pallas kernels, final_pass(): pl.pallas_call(functools.partial(final_kernel, shape), name='final', out_...  8.94 us

profile of v2, /device:TPU:1, one launch (start us, length us, event | category | flops | bytes accessed | tf_op | source)
XLA Modules:
  0.0 45.1 jit_solution(1973248927457889795)
XLA Ops:
  0.0 0.0 copy-start
  0.0 36.1 %local.1 = (f32[64,16,8,256]{3,2,1,0:T(8,128)S(1)}, f32[66,16,8,256]{3,2,1,0:T(8,128)S(1)}, f32[2,64,8,256]{3,2,1,0:T(8,128)S(1)}, f32[64,8,128]{2,1,0:T(8,128)S...) custom-call(f32[64,128,256]{2,1,0:T(8,128)} %u_ref.1, ...), custom_call_target="tpu_custom_call" | custom-call | tf_op jit(solution)/shard_map/local/pallas_call | solution.py:554
  36.2 0.0 copy-done
  36.2 8.9 %final.1 = f32[64,128,256]{2,1,0:T(8,128)} custom-call(f32[64,16,8,256]{3,2,1,0:T(8,128)S(1)} %get-tuple-element.13.g_v, f32[66,16,8,256]{3,2,1,0:T(8,128)S(1)} %get-tuple-element.14.u_v, f32[2,64,8,256]{3,2,1,0:T(8,128)S(1)} %get-tuple-element.15.sg_ref, f32[64,8,128]{2,1,0:T(8,128)S(1)} %get-tuple-element.16.cz_ref, ...), custom_call_target="tpu_custom_call" | custom-call | tf_op jit(solution)/shard_map/final/pallas_call | solution.py:687
Async XLA Ops:
  0.0 36.2 %copy-start = (f32[2,512]{1,0:T(2,128)S(1)}, f32[2,512]{1,0:T(2,128)}, u32[]{:S(2)}) copy-start(f32[2,512]{1,0:T(2,128)} %constant.29.clone.xtab_ref) | copy-start | bytes 12292

commit v3 on v2

--- a/solution.py
+++ b/solution.py
@@ -82,7 +82,7 @@
     uh, ul = split_bf16(zu)
     vh, vl = split_bf16(zv)
     zero = np.zeros_like(uh)
-    tables["zmom"] = np.stack([uh, ul, vh, vl] + [zero] * 12, 1)
+    tables["zmom"] = np.stack([uh, ul, vh, vl] + [zero] * (LANES - 4), 2)
     tables["zadd"] = np.stack([vh, vh, vl, uh, uh, ul, zero, zero], 1)
     return tables
 
@@ -151,7 +151,7 @@
     g_v, u_v, sg_ref, cz_ref, cy_ref, cx_ref, ytab_ref, zadd_ref,
     bz_ref, zmom_ref, yw_ref, xw_ref, wy_ref, by_ref, bx_ref, tsem,
     s_v, fh0, fl0, fh1, fl1, y0, y1, hy, mxf, mxu, mx, my, mz,
-    zbuf, zpad, ybuf, xpair, xtot, xbuf, xback, eown, ebuf, qown, qbuf, rown, rbuf, town, tbuf,
+    zbuf, zpad, ybuf, xpair, xtot, xbuf, xback, eown, ebuf, qown, qbuf, rown, rbuf, town, tbuf, face,
     usem, ssem, hs, hr, zs, zr, ys, yr, ps, pr, xs, xr, bs, br, es, er, qs, qr, rs, rr, ts, tr,
 ):
     gx, gy, gz = lax.axis_index("gx"), lax.axis_index("gy"), lax.axis_index("gz")
@@ -191,10 +191,6 @@
     for b in early + [b for b in range(blocks) if b not in early]:
         for copy in u_loads(b):
             copy.start()
-    for b in range(blocks):
-        for copy in s_loads(b):
-            copy.start()
-
     table_loads = [
         pltpu.make_async_copy(hbm.at[index], ref, tsem.at[n])
         for n, (hbm, index, ref) in enumerate((
@@ -225,6 +221,9 @@
             copy.wait()
     for copy in halos[2:]:
         copy.start()
+    for b in range(blocks):
+        for copy in s_loads(b):
+            copy.start()
 
     sub = lax.broadcasted_iota(jnp.int32, (SUB, LANES), 0)
 
@@ -282,15 +281,12 @@
     halves = ((fh0, fl0), (fh1, fl1))
 
     def z_moments(source, k, c):
-        mom = None
-        for f in source:
-            flat = f[k].reshape(PLANES * north, upward)
-            part = lax.dot_general(zmom, flat, NT, preferred_element_type=F32)
-            mom = part if mom is None else mom + part
+        flat = jnp.concatenate([f[k].reshape(PLANES * north, upward) for f in source], 1)
+        mom = jnp.dot(flat, jnp.concatenate([zmom, zmom], 0), preferred_element_type=F32)
+        across = [mom[p * north:(p + 1) * north].T for p in range(PLANES)]
         for kind in range(2):
-            m = mom[2 * kind:2 * kind + 1] + mom[2 * kind + 1:2 * kind + 2]
             mz[kind, pl.ds(pl.multiple_of(c * PLANES, PLANES), PLANES), :] = stack_rows(
-                [m[:, p * north:(p + 1) * north] for p in range(PLANES)])
+                [a[2 * kind:2 * kind + 1] + a[2 * kind + 1:2 * kind + 2] for a in across])
 
     def rhs(target, k, c):
         high_ref, low_ref = target
@@ -407,6 +403,58 @@
         for copy in rcopies:
             copy.start()
 
+    ecopies = [
+        remote(eown.at[kind_to(gy, ny, o)], ebuf.at[o - 1], es.at[o - 1], er.at[o - 1],
+               at("gy", lax.rem(gy + o, ny)))
+        for o in range(1, ny)
+    ]
+    tcopies = [
+        remote(town.at[kind_to(gx, nx, o)], tbuf.at[o - 1], ts.at[o - 1], tr.at[o - 1],
+               at("gx", lax.rem(gx + o, nx)))
+        for o in range(1, nx)
+    ]
+
+    def z_rows():
+        for copy in zcopies:
+            copy.wait()
+        for m, value in enumerate(gather(gz, nz, zbuf)):
+            zpad[m, 0:east] = value
+        for kind in range(2):
+            eown[kind] = dot(yw_ref[kind, 0], zpad[0], NT) + dot(yw_ref[kind, 1], zpad[1], NT)
+        for copy in ecopies:
+            copy.start()
+        for m in range(2):
+            face[m] = dot(zpad[m, 0:east], by_ref[...])
+
+    def z_planes():
+        for copy in ecopies:
+            copy.wait()
+        eleft, eright = gather(gy, ny, ebuf)
+        value = [
+            face[m] + (dot(eleft, yw_ref[1, m], TN) + dot(eright, yw_ref[0, m], TN))[0:east]
+            for m in range(2)
+        ]
+        for kind in range(2):
+            town[kind] = dot(xw_ref[kind, 0], value[0]) + dot(xw_ref[kind, 1], value[1])
+        for copy in tcopies:
+            copy.start()
+        for m in range(2):
+            face[m] = dot(bx_ref[...], value[m])
+
+    part = east // 2
+    ycopies = [
+        [
+            remote(my.at[kind_to(gy, ny, o), pl.ds(n * part, part)], ybuf.at[o - 1, pl.ds(n * part, part)],
+                   ys.at[n, o - 1], yr.at[n, o - 1], at("gy", lax.rem(gy + o, ny)))
+            for o in range(1, ny)
+        ]
+        for n in range(2)
+    ]
+
+    def send_rows(n):
+        for copy in ycopies[n]:
+            copy.start()
+
     def multiply(source, k, target):
         high_ref, low_ref = source
         target[...] = solve_up(
@@ -438,8 +486,13 @@
         def _():
             send_chips()
 
+        @pl.when(k == max(pairs - 2, 0))
+        def _():
+            z_rows()
+
         @pl.when(k == pairs - 1)
         def _():
+            send_rows(0)
             send_edges()
 
         multiply(halves[0], k, y0)
@@ -451,47 +504,8 @@
     lax.fori_loop(0, pairs, solve_pair, 0)
     finish(y1, chunks - 1)
 
-    for copy in zcopies:
-        copy.wait()
-    coef = gather(gz, nz, zbuf)
-    for m in range(2):
-        zpad[m, 0:east] = coef[m]
-    for kind in range(2):
-        eown[kind] = dot(yw_ref[kind, 0], zpad[0], NT) + dot(yw_ref[kind, 1], zpad[1], NT)
-    ecopies = [
-        remote(eown.at[kind_to(gy, ny, o)], ebuf.at[o - 1], es.at[o - 1], er.at[o - 1],
-               at("gy", lax.rem(gy + o, ny)))
-        for o in range(1, ny)
-    ]
-    for copy in ecopies:
-        copy.start()
-    ycopies = [
-        remote(my.at[kind_to(gy, ny, o)], ybuf.at[o - 1], ys.at[o - 1], yr.at[o - 1],
-               at("gy", lax.rem(gy + o, ny)))
-        for o in range(1, ny)
-    ]
-    for copy in ycopies:
-        copy.start()
-
-    by = by_ref[...]
-    face = [dot(coef[m], by) for m in range(2)]
-    for copy in ecopies:
-        copy.wait()
-    eleft, eright = gather(gy, ny, ebuf)
-    for m in range(2):
-        face[m] = face[m] + (
-            dot(eleft, yw_ref[1, m], TN) + dot(eright, yw_ref[0, m], TN))[0:east]
-    for kind in range(2):
-        town[kind] = dot(xw_ref[kind, 0], face[0]) + dot(xw_ref[kind, 1], face[1])
-    tcopies = [
-        remote(town.at[kind_to(gx, nx, o)], tbuf.at[o - 1], ts.at[o - 1], tr.at[o - 1],
-               at("gx", lax.rem(gx + o, nx)))
-        for o in range(1, nx)
-    ]
-    for copy in tcopies:
-        copy.start()
-    bx = bx_ref[...]
-    face = [dot(bx, face[m]) for m in range(2)]
+    send_rows(1)
+    z_planes()
 
     for copy in xcopies:
         copy.wait()
@@ -510,6 +524,7 @@
     rright = rright + rown[1]
     back.wait()
     wy = wy_ref[...]
+    by = by_ref[...]
     cx_ref[0] = dot(by, cx_ref[0]) + dot(wy, rleft, TN)
     cx_ref[1] = dot(by, cx_ref[1] + mx[1]) + dot(wy, rright, TN)
 
@@ -524,8 +539,9 @@
         cz_ref[:, 3 * m + 2, :] = high
         cz_ref[:, 6 + m, :] = jnp.zeros_like(value)
 
-    for copy in ycopies:
-        copy.wait()
+    for n in range(2):
+        for copy in ycopies[n]:
+            copy.wait()
     left, right = gather(gy, ny, ybuf)
     cy_ref[0] = left
     cy_ref[1] = right
@@ -567,7 +583,7 @@
         in_specs=[hbm, hbm] + [hbm] * len(names) + [smem],
         out_specs=(vmem,) * 8,
         scratch_shapes=[
-            pltpu.VMEM((2, upward, upward), BF16), pltpu.VMEM((16, upward), BF16),
+            pltpu.VMEM((2, upward, upward), BF16), pltpu.VMEM((upward, LANES), BF16),
             buf(2, 2, SUB, north), buf(2, 2, SUB, east), buf(SUB, north), buf(north, north), buf(east, east),
             dma((len(names),)),
             buf(east, steps, SUB, upward),
@@ -581,11 +597,11 @@
             buf(2, SUB, LANES), buf(ny - 1, SUB, LANES),
             buf(2, SUB, upward), buf(ny - 1, SUB, upward),
             buf(2, SUB, upward), buf(nx - 1, SUB, upward),
-            buf(2, SUB, north), buf(nx - 1, SUB, north),
+            buf(2, SUB, north), buf(nx - 1, SUB, north), buf(2, east, north),
             dma((blocks, SUB)), dma((blocks, SUB)),
             dma((4,)), dma((4,)),
             dma((nz - 1,)), dma((nz - 1,)),
-            dma((ny - 1,)), dma((ny - 1,)),
+            dma((2, ny - 1)), dma((2, ny - 1)),
             dma, dma,
             dma((chips - 1,)), dma((chips - 1,)),
             dma, dma,

time: 45.2 us -> 42.9 us (0.949)
  Pallas kernels: 45.1 us -> 42.7 us
    pallas_call x1, Pallas kernels: 36.1 us -> 33.8 us  [local_pass(): pl.pallas_call(functools.partial(local_kernel, sizes, u.shape, tables['fa...]
where the time goes in v3:
time: 42.9 us; the launch traced here: 42.7 us
  Pallas kernels  42.7 us (100%)
    pallas_call x1, Pallas kernels, local_pass(): pl.pallas_call(functools.partial(local_kernel, sizes, u.shape, tables['fa...  33.8 us
    pallas_call x1, Pallas kernels, final_pass(): pl.pallas_call(functools.partial(final_kernel, shape), name='final', out_...  8.94 us

profile of v3, /device:TPU:1, one launch (start us, length us, event | category | flops | bytes accessed | tf_op | source)
XLA Modules:
  0.0 42.7 jit_solution(7806560662308496997)
XLA Ops:
  0.0 0.0 copy-start
  0.0 33.8 %local.1 = (f32[64,16,8,256]{3,2,1,0:T(8,128)S(1)}, f32[66,16,8,256]{3,2,1,0:T(8,128)S(1)}, f32[2,64,8,256]{3,2,1,0:T(8,128)S(1)}, f32[64,8,128]{2,1,0:T(8,128)S...) custom-call(f32[64,128,256]{2,1,0:T(8,128)} %u_ref.1, ...), custom_call_target="tpu_custom_call" | custom-call | tf_op jit(solution)/shard_map/local/pallas_call | solution.py:570
  33.8 0.0 copy-done
  33.8 8.9 %final.1 = f32[64,128,256]{2,1,0:T(8,128)} custom-call(f32[64,16,8,256]{3,2,1,0:T(8,128)S(1)} %get-tuple-element.13.g_v, f32[66,16,8,256]{3,2,1,0:T(8,128)S(1)} %get-tuple-element.14.u_v, f32[2,64,8,256]{3,2,1,0:T(8,128)S(1)} %get-tuple-element.15.sg_ref, f32[64,8,128]{2,1,0:T(8,128)S(1)} %get-tuple-element.16.cz_ref, ...), custom_call_target="tpu_custom_call" | custom-call | tf_op jit(solution)/shard_map/final/pallas_call | solution.py:703
Async XLA Ops:
  0.0 33.8 %copy-start = (f32[2,512]{1,0:T(2,128)S(1)}, f32[2,512]{1,0:T(2,128)}, u32[]{:S(2)}) copy-start(f32[2,512]{1,0:T(2,128)} %constant.29.clone.xtab_ref) | copy-start | bytes 12292

commit v4 on v3

--- a/solution.py
+++ b/solution.py
@@ -71,10 +71,10 @@
         for kind, w in enumerate((ux, vx)):
             xw[:, kind, slot, slot] = w.reshape(members[0], east)
     tables["yw"], tables["xw"] = yw, xw
-    wy = np.zeros((members[1], SUB, north), np.float32)
-    wy[:, 0] = own[:, 1]
-    wy[:, 1] = own[:, 0]
-    tables["wy"] = wy
+    yuh, yul = [a.astype(np.float32) for a in split_bf16(own[:, 0].astype(np.float64))]
+    yvh, yvl = [a.astype(np.float32) for a in split_bf16(own[:, 1].astype(np.float64))]
+    zero = np.zeros_like(yuh)
+    tables["yadd"] = np.stack([yvh, yvl, yvh, yuh, yul, yuh, zero, zero], 1)
 
     bzh, bzl = split_bf16(diagonal_blocks(uz, vz, members[2]))
     tables["bz"] = np.stack([bzh, bzl], 1)
@@ -147,10 +147,10 @@
 
 def local_kernel(
     sizes, shape, factors,
-    u_ref, s_ref, bz_hbm, zmom_hbm, ytab_hbm, yw_hbm, xw_hbm, wy_hbm, by_hbm, bx_hbm, zadd_hbm, xtab_ref,
-    g_v, u_v, sg_ref, cz_ref, cy_ref, cx_ref, ytab_ref, zadd_ref,
-    bz_ref, zmom_ref, yw_ref, xw_ref, wy_ref, by_ref, bx_ref, tsem,
-    s_v, fh0, fl0, fh1, fl1, y0, y1, hy, mxf, mxu, mx, my, mz,
+    u_ref, s_ref, bz_hbm, zmom_hbm, ytab_hbm, yw_hbm, xw_hbm, by_hbm, bx_hbm, zadd_hbm, xtab_ref,
+    g_v, cz_ref, cy_ref, cx_ref, zadd_ref,
+    bz_ref, zmom_ref, yw_ref, xw_ref, by_ref, bx_ref, tsem,
+    u_v, sg_ref, ytab_ref, edge_v, xland, s_v, fh0, fl0, fh1, fl1, y0, y1, hy, mxf, mxu, mx, my, mz,
     zbuf, zpad, ybuf, xpair, xtot, xbuf, xback, eown, ebuf, qown, qbuf, rown, rbuf, town, tbuf, face,
     usem, ssem, hs, hr, zs, zr, ys, yr, ps, pr, xs, xr, bs, br, es, er, qs, qr, rs, rr, ts, tr,
 ):
@@ -195,7 +195,7 @@
         pltpu.make_async_copy(hbm.at[index], ref, tsem.at[n])
         for n, (hbm, index, ref) in enumerate((
             (bz_hbm, gz, bz_ref), (zmom_hbm, gz, zmom_ref), (ytab_hbm, gy, ytab_ref), (yw_hbm, gy, yw_ref),
-            (xw_hbm, gx, xw_ref), (wy_hbm, gy, wy_ref), (by_hbm, gy, by_ref), (bx_hbm, gx, bx_ref),
+            (xw_hbm, gx, xw_ref), (by_hbm, gy, by_ref), (bx_hbm, gx, bx_ref),
             (zadd_hbm, gz, zadd_ref)))
     ]
     for copy in table_loads:
@@ -441,10 +441,11 @@
         for m in range(2):
             face[m] = dot(bx_ref[...], value[m])
 
-    part = east // 2
+    parts = (max(chunks - 3, 1) * PLANES, east)
     ycopies = [
         [
-            remote(my.at[kind_to(gy, ny, o), pl.ds(n * part, part)], ybuf.at[o - 1, pl.ds(n * part, part)],
+            remote(my.at[kind_to(gy, ny, o), pl.ds(n * parts[0], parts[n] - n * parts[0])],
+                   ybuf.at[o - 1, pl.ds(n * parts[0], parts[n] - n * parts[0])],
                    ys.at[n, o - 1], yr.at[n, o - 1], at("gy", lax.rem(gy + o, ny)))
             for o in range(1, ny)
         ]
@@ -507,26 +508,71 @@
     send_rows(1)
     z_planes()
 
-    for copy in xcopies:
-        copy.wait()
-    px, sx = gather(chip, chips, xbuf)
+    by = by_ref[...]
+    edge_v[0] = jnp.zeros((north, upward), F32)
+    edge_v[1] = dot(by, mx[1])
+
+    def scan(value, backward):
+        def shifted(x, d):
+            if backward:
+                return jnp.where(sub < SUB - d, pltpu.roll(x, SUB - d, 0), 0.0)
+            return jnp.where(sub >= d, pltpu.roll(x, d, 0), 0.0)
+
+        for d in (1, 2, 4):
+            value = value + shifted(value, d)
+        return shifted(value, 1)
+
     first = jnp.where(core == 0, 1.0, 0.0).astype(F32)
     second = 1.0 - first
-    xback[0] = px + first * mx[0, mine, :]
-    xback[1] = sx + second * mx[1, mine, :]
-    back = remote(xback, cx_ref.at[:, mine, :], bs, br, partner)
-    back.start()
-    cx_ref[0, mine, :] = px + second * xpair[0]
-    cx_ref[1, mine, :] = sx + first * xpair[1]
-    for copy in rcopies:
-        copy.wait()
-    rleft, rright = gather(gx, nx, rbuf)
-    rright = rright + rown[1]
+    back = remote(xback, xland, bs, br, partner)
+
+    def return_chips():
+        for copy in xcopies:
+            copy.wait()
+        px, sx = gather(chip, chips, xbuf)
+        xback[0] = px + first * mx[0, mine, :]
+        xback[1] = sx + second * mx[1, mine, :]
+        back.start()
+        cx_ref[0, mine, :] = px + second * xpair[0]
+        cx_ref[1, mine, :] = sx + first * xpair[1]
+
+    def sweep(c, carry):
+        @pl.when(c == min(2, chunks - 1))
+        def _():
+            return_chips()
+
+        base = pl.multiple_of(c * PLANES, PLANES)
+        wx = weights(base)
+        for l in range(tiles):
+            col = cols(l)
+            low, high = [], []
+            for p in range(PLANES):
+                su, sv = sg_ref[0, base + p, :, col], sg_ref[1, base + p, :, col]
+                low.append(scan(su, False))
+                high.append(scan(sv, True) + sv)
+            for t in range(steps):
+                wu, wv = ytab_ref[0, rows_at(t)], ytab_ref[1, rows_at(t)]
+                below, above = edge_v[0, rows_at(t), col], edge_v[1, rows_at(t), col]
+                for p in range(PLANES):
+                    i = base + p
+                    g = g_v[i, t, :, col]
+                    low[p] = low[p] + wu * g
+                    high[p] = high[p] - wv * g
+                    h = wv * low[p] + wu * high[p]
+                    below = below + wx[0][p] * h
+                    above = above - wx[1][p] * h
+                    g_v[i, t, :, col] = u_v[i + 1, t, :, col] + (wx[1][p] * below + wx[0][p] * above)
+                edge_v[0, rows_at(t), col] = below
+                edge_v[1, rows_at(t), col] = above
+        return carry
+
+    lax.fori_loop(0, chunks, sweep, 0)
+
     back.wait()
-    wy = wy_ref[...]
-    by = by_ref[...]
-    cx_ref[0] = dot(by, cx_ref[0]) + dot(wy, rleft, TN)
-    cx_ref[1] = dot(by, cx_ref[1] + mx[1]) + dot(wy, rright, TN)
+    cx_ref[0, theirs, :] = xland[0]
+    cx_ref[1, theirs, :] = xland[1]
+    cx_ref[0] = dot(by, cx_ref[0])
+    cx_ref[1] = dot(by, cx_ref[1])
 
     for copy in tcopies:
         copy.wait()
@@ -539,12 +585,20 @@
         cz_ref[:, 3 * m + 2, :] = high
         cz_ref[:, 6 + m, :] = jnp.zeros_like(value)
 
+    for copy in rcopies:
+        copy.wait()
+    rleft, rright = gather(gx, nx, rbuf)
+    fixed = [dot(xw_ref[1, m], rleft, TN) + dot(xw_ref[0, m], rright, TN) for m in range(2)]
     for n in range(2):
         for copy in ycopies[n]:
             copy.wait()
-    left, right = gather(gy, ny, ybuf)
-    cy_ref[0] = left
-    cy_ref[1] = right
+    for m, face_y in enumerate(gather(gy, ny, ybuf)):
+        value = dot(bx_ref[...], face_y) + fixed[m]
+        high = value.astype(BF16).astype(F32)
+        cy_ref[:, 3 * m, :] = high
+        cy_ref[:, 3 * m + 1, :] = high
+        cy_ref[:, 3 * m + 2, :] = (value - high).astype(BF16).astype(F32)
+        cy_ref[:, 6 + m, :] = jnp.zeros_like(value)
 
 
 def local_pass(u, s, tables, sizes):
@@ -566,26 +620,28 @@
     def halves():
         return pltpu.VMEM((pairs, PLANES, north, upward), BF16)
 
-    names = ("bz", "zmom", "y", "yw", "xw", "wy", "by", "bx", "zadd")
+    names = ("bz", "zmom", "y", "yw", "xw", "by", "bx", "zadd")
     return pl.pallas_call(
         functools.partial(local_kernel, sizes, u.shape, tables["factors"]),
         name="local",
         out_shape=(
             buf(east, steps, SUB, upward),
-            buf(east + 2, steps, SUB, upward),
-            buf(2, east, SUB, upward),
             buf(east, SUB, north),
-            buf(2, east, upward),
+            buf(east, SUB, upward),
             buf(2, north, upward),
-            buf(2, north, LANES),
             pltpu.VMEM((SUB, upward), BF16),
         ),
         in_specs=[hbm, hbm] + [hbm] * len(names) + [smem],
-        out_specs=(vmem,) * 8,
+        out_specs=(vmem,) * 5,
         scratch_shapes=[
             pltpu.VMEM((2, upward, upward), BF16), pltpu.VMEM((upward, LANES), BF16),
-            buf(2, 2, SUB, north), buf(2, 2, SUB, east), buf(SUB, north), buf(north, north), buf(east, east),
+            buf(2, 2, SUB, north), buf(2, 2, SUB, east), buf(north, north), buf(east, east),
             dma((len(names),)),
+            buf(east + 2, steps, SUB, upward),
+            buf(2, east, SUB, upward),
+            buf(2, north, LANES),
+            buf(2, north, upward),
+            buf(2, half, upward),
             buf(east, steps, SUB, upward),
             halves(), halves(), halves(), halves(),
             buf(PLANES * north, upward), buf(PLANES * north, upward),
@@ -615,17 +671,17 @@
     )(*[pltpu.with_memory_space_constraint(a, pltpu.HBM) for a in [u, s] + [tables[name] for name in names + ("x",)]])
 
 
-LOCAL_VMEM = 34 * 2**20
+LOCAL_VMEM = 44 * 2**20
 FINAL_VMEM = 24 * 2**20
 
 
 def final_kernel(
     shape,
-    g_v, u_v, sg_ref, cz_ref, cy_ref, cx_ref, zadd_ref, ytab_ref, xtab_ref,
+    t_v, cz_ref, cy_ref, cx_ref, zadd_ref, yadd_ref, xtab_ref,
     o_ref,
-    edge_v, o_v, osem,
+    o_v, osem,
 ):
-    gx, gy, gz = lax.axis_index("gx"), lax.axis_index("gy"), lax.axis_index("gz")
+    gx, gy = lax.axis_index("gx"), lax.axis_index("gy")
     east, north, upward = shape
     tiles = upward // LANES
     steps = north // SUB
@@ -639,51 +695,25 @@
             for k in range(SUB)
         ]
 
-    edge_v[...] = cx_ref[...]
-    zadd = zadd_ref[...]
-    sub = lax.broadcasted_iota(jnp.int32, (SUB, LANES), 0)
-
-    def scan(value, backward):
-        def shifted(x, d):
-            if backward:
-                return jnp.where(sub < SUB - d, pltpu.roll(x, SUB - d, 0), 0.0)
-            return jnp.where(sub >= d, pltpu.roll(x, d, 0), 0.0)
-
-        for d in (1, 2, 4):
-            value = value + shifted(value, d)
-        return shifted(value, 1)
+    zadd = zadd_ref[...].astype(F32)
+    yadd = yadd_ref[gy]
 
     def step(c, carry):
         base = pl.multiple_of(c * PLANES, PLANES)
         wx = [[xtab_ref[kind, gx * east + base + p] for p in range(PLANES)] for kind in range(2)]
         add = []
         for p in range(PLANES):
-            cz = cz_ref[base + p].T.astype(BF16)
-            add.append(jnp.dot(cz, zadd, preferred_element_type=F32))
+            left = jnp.concatenate([cz_ref[base + p], yadd], 0).T.astype(BF16)
+            right = jnp.concatenate([zadd, cy_ref[base + p]], 0).astype(BF16)
+            add.append(jnp.dot(left, right, preferred_element_type=F32))
         for l in range(tiles):
             col = slice(l * LANES, (l + 1) * LANES)
-            edge = [cy_ref[kind, pl.ds(base, PLANES), col] for kind in range(2)]
-            low, high = [], []
-            for p in range(PLANES):
-                su, sv = sg_ref[0, base + p, :, col], sg_ref[1, base + p, :, col]
-                low.append(scan(su, False) + edge[0][p:p + 1])
-                high.append(scan(sv, True) + edge[1][p:p + 1] + sv)
             for t in range(steps):
                 row = slice(t * SUB, (t + 1) * SUB)
-                wu, wv = ytab_ref[0, row], ytab_ref[1, row]
-                below, above = edge_v[0, row, col], edge_v[1, row, col]
+                below, above = cx_ref[0, row, col], cx_ref[1, row, col]
                 for p in range(PLANES):
-                    i = base + p
-                    g = g_v[i, t, :, col]
-                    low[p] = low[p] + wu * g
-                    high[p] = high[p] - wv * g
-                    h = wv * low[p] + wu * high[p]
-                    below = below + wx[0][p] * h
-                    above = above - wx[1][p] * h
-                    o_v[i, t, :, col] = (
-                        u_v[i + 1, t, :, col] + add[p][row, col] + (wx[1][p] * below + wx[0][p] * above))
-                edge_v[0, row, col] = below
-                edge_v[1, row, col] = above
+                    o_v[base + p, t, :, col] = (t_v[base + p, t, :, col] + add[p][row, col]) + (
+                        wx[1][p] * below + wx[0][p] * above)
         for copy in stores(c):
             copy.start()
         return carry
@@ -694,7 +724,7 @@
             copy.wait()
 
 
-def final_pass(g, u, sg, cz, cy, cx, ytab, zadd, tables, shape):
+def final_pass(t, cz, cy, cx, zadd, tables, shape):
     east, north, upward = shape
     steps = north // SUB
     chunks = east // PLANES
@@ -704,21 +734,19 @@
         functools.partial(final_kernel, shape),
         name="final",
         out_shape=jax.ShapeDtypeStruct(shape, F32),
-        in_specs=[vmem] * 8 + [smem],
+        in_specs=[vmem] * 6 + [smem],
         out_specs=pl.BlockSpec(memory_space=pl.ANY),
         scratch_shapes=[
-            pltpu.VMEM((2, north, upward), F32),
             pltpu.VMEM((east, steps, SUB, upward), F32),
             pltpu.SemaphoreType.DMA((chunks, SUB)),
         ],
         compiler_params=pltpu.CompilerParams(vmem_limit_bytes=FINAL_VMEM),
-    )(g, u, sg, cz, cy, cx, zadd, ytab, tables["x"])
+    )(t, cz, cy, cx, zadd, tables["yadd"], tables["x"])
 
 
 def local(sizes, u, s):
     tables = make_tables(u.shape, sizes)
-    g, padded, *faces = local_pass(u, s, tables, sizes)
-    return final_pass(g, padded, *faces, tables, u.shape)
+    return final_pass(*local_pass(u, s, tables, sizes), tables, u.shape)
 
 
 def solution(mesh):

time: 42.9 us -> 40.5 us (0.944); the launches traced: 42.7 us -> 39.8 us
  Pallas kernels: 42.7 us -> 39.8 us
    pallas_call x1, Pallas kernels: 8.94 us -> 5.5 us  [final_pass(): pl.pallas_call(functools.partial(final_kernel, shape), name='final', out_...]
    pallas_call x1, Pallas kernels: 33.8 us -> 34.3 us  [local_pass(): pl.pallas_call(functools.partial(local_kernel, sizes, u.shape, tables['fa...]
where the time goes in v4:
time: 40.5 us; the launch traced here: 39.8 us
  Pallas kernels  39.8 us (98%)
    pallas_call x1, Pallas kernels, local_pass(): pl.pallas_call(functools.partial(local_kernel, sizes, u.shape, tables['fa...  34.3 us
    pallas_call x1, Pallas kernels, final_pass(): pl.pallas_call(functools.partial(final_kernel, shape), name='final', out_...  5.5 us

profile of v4, /device:TPU:1, one launch (start us, length us, event | category | flops | bytes accessed | tf_op | source)
XLA Modules:
  0.0 39.8 jit_solution(16082993523669893522)
XLA Ops:
  0.0 0.0 copy-start
  0.0 0.0 copy-start.1
  0.0 34.3 %local.1 = (f32[64,16,8,256]{3,2,1,0:T(8,128)S(1)}, f32[64,8,128]{2,1,0:T(8,128)S(1)}, f32[64,8,256]{2,1,0:T(8,128)S(1)}, f32[2,128,256]{2,1,0:T(8,128)S(1)}, bf16[8,256]{1,0:T(8,128)(2,1)S(1)}) custom-call(f32[64,128,256]{2,1,0:T(8,128)} %u_ref.1, f32[64,128,256]{2,1,0:T(8,128)} %s_ref.1, bf16[4,2,256,256]{3,2,1,0:T(8,128)(2,1)} %constant.20.clone.bz_hbm, ...), custom_call_target="tpu_custom_call" | custom-call | tf_op jit(solution)/shard_map/local/pallas_call | solution.py:624
  34.3 0.0 copy-done
  34.3 0.0 copy-done.1
  34.3 5.5 %final.1 = f32[64,128,256]{2,1,0:T(8,128)} custom-call(f32[64,16,8,256]{3,2,1,0:T(8,128)S(1)} %get-tuple-element.10.t_v, f32[64,8,128]{2,1,0:T(8,128)S(1)} %get-tuple-element.11.cz_ref, f32[64,8,256]{2,1,0:T(8,128)S(1)} %get-tuple-element.12.cy_ref, f32[2,128,256]{2,1,0:T(8,128)S(1)} %get-tuple-element.13.cx_ref, ...), custom_call_target="tpu_custom_call" | custom-call | tf_op jit(solution)/shard_map/final/pallas_call | solution.py:733
Async XLA Ops:
  0.0 34.3 %copy-start = (f32[4,8,128]{2,1,0:T(8,128)S(1)}, f32[4,8,128]{2,1,0:T(8,128)}, u32[]{:S(2)}) copy-start(f32[4,8,128]{2,1,0:T(8,128)} %constant.29.clone.yadd_ref) | copy-start | bytes 49156
  0.0 34.3 %copy-start.1 = (f32[2,512]{1,0:T(2,128)S(1)}, f32[2,512]{1,0:T(2,128)}, u32[]{:S(2)}) copy-start(f32[2,512]{1,0:T(2,128)} %constant.28.clone.xtab_ref) | copy-start | bytes 12292

commit v5 on v4

--- a/solution.py
+++ b/solution.py
@@ -124,10 +124,12 @@
 
 
 def dot(a, b, dims=NN):
-    if dims == TN:
-        return lax.dot_general(a, b, dims, precision=HIGH, preferred_element_type=F32)
     ah, al = split(a)
     bh, bl = split(b)
+    if dims == TN:
+        parts = [[x.astype(F32) for x in group] for group in ((ah, al, ah), (bl, bh, bh))]
+        left, right = (jnp.concatenate(group + [jnp.zeros_like(group[0])], 0).astype(BF16) for group in parts)
+        return lax.dot_general(left, right, dims, preferred_element_type=F32)
     left = jnp.concatenate([ah, al, ah], 1)
     right = jnp.concatenate([bl, bh, bh], dims[0][1][0])
     return lax.dot_general(left, right, dims, preferred_element_type=F32)

time: 40.5 us -> 39.9 us (0.985)
  Pallas kernels: 39.8 us -> 39.2 us
    pallas_call x1, Pallas kernels: 34.3 us -> 33.7 us  [local_pass(): pl.pallas_call(functools.partial(local_kernel, sizes, u.shape, tables['fa...]
where the time goes in v5:
time: 39.9 us; the launch traced here: 39.2 us
  Pallas kernels  39.2 us (98%)
    pallas_call x1, Pallas kernels, local_pass(): pl.pallas_call(functools.partial(local_kernel, sizes, u.shape, tables['fa...  33.7 us
    pallas_call x1, Pallas kernels, final_pass(): pl.pallas_call(functools.partial(final_kernel, shape), name='final', out_...  5.5 us

profile of v5, /device:TPU:1, one launch (start us, length us, event | category | flops | bytes accessed | tf_op | source)
XLA Modules:
  0.0 39.2 jit_solution(4566893167494467177)
XLA Ops:
  0.0 0.0 copy-start
  0.0 0.0 copy-start.1
  0.0 33.7 %local.1 = (f32[64,16,8,256]{3,2,1,0:T(8,128)S(1)}, f32[64,8,128]{2,1,0:T(8,128)S(1)}, f32[64,8,256]{2,1,0:T(8,128)S(1)}, f32[2,128,256]{2,1,0:T(8,128)S(1)}, bf16[8,256]{1,0:T(8,128)(2,1)S(1)}) custom-call(f32[64,128,256]{2,1,0:T(8,128)} %u_ref.1, f32[64,128,256]{2,1,0:T(8,128)} %s_ref.1, bf16[4,2,256,256]{3,2,1,0:T(8,128)(2,1)} %constant.20.clone.bz_hbm, ...), custom_call_target="tpu_custom_call" | custom-call | tf_op jit(solution)/shard_map/local/pallas_call | solution.py:626
  33.7 0.0 copy-done
  33.7 0.0 copy-done.1
  33.7 5.5 %final.1 = f32[64,128,256]{2,1,0:T(8,128)} custom-call(f32[64,16,8,256]{3,2,1,0:T(8,128)S(1)} %get-tuple-element.10.t_v, f32[64,8,128]{2,1,0:T(8,128)S(1)} %get-tuple-element.11.cz_ref, f32[64,8,256]{2,1,0:T(8,128)S(1)} %get-tuple-element.12.cy_ref, f32[2,128,256]{2,1,0:T(8,128)S(1)} %get-tuple-element.13.cx_ref, ...), custom_call_target="tpu_custom_call" | custom-call | tf_op jit(solution)/shard_map/final/pallas_call | solution.py:735
Async XLA Ops:
  0.0 33.7 %copy-start = (f32[4,8,128]{2,1,0:T(8,128)S(1)}, f32[4,8,128]{2,1,0:T(8,128)}, u32[]{:S(2)}) copy-start(f32[4,8,128]{2,1,0:T(8,128)} %constant.29.clone.yadd_ref) | copy-start | bytes 49156
  0.0 33.7 %copy-start.1 = (f32[2,512]{1,0:T(2,128)S(1)}, f32[2,512]{1,0:T(2,128)}, u32[]{:S(2)}) copy-start(f32[2,512]{1,0:T(2,128)} %constant.28.clone.xtab_ref) | copy-start | bytes 12292
